TPU v7x, 128 devices: a whole 4x4x4 slice. The times are simulated.
128 devices in a mesh: row: 16 (over y, x), col: 8 (over z, core).
Axes of the slice: x: 4, y: 4, z: 4, core: 2. Of those that a mesh axis runs over, the one named last changes fastest.
Arguments:
- spectra: bfloat16 [16384, 4096], P(('row', 'col')), may hold values from 0 to 16, as said below
- projection: bfloat16 [4096, 1024], replicated, may hold values from -0.09375 to 0.09375
- kernel_slot: int32 [16384], P(('row', 'col')), may hold values from 0 to 16383, as said below
- env_image: int32 [16384], P(('row', 'col')), may hold values from 0 to 1023, never falling along the last dimension, each value on 1 to 48 neighbouring positions
- image_atoms: int32 [1024], replicated, may hold values from 8 to 64
Outputs:
- panels: float32 [16384, 1024], P('row')
- trailing: float32 [16384, 16384], P('row', 'col')
Inputs may be any that keep to these rules, and one draw needn't show every extreme that they name: `spectra`: Nonnegative. A permutation. With the block of environment e being kernel_slot[e] // 128: among the 128 environments of one device (aligned blocks of 128 in environment order) at most 1 fall in any one block, and in every draw some block receives 1 of them.
All inputs are finite; a program needn't handle non-finite values.
Results may differ from a plain program's by a relative error of at most 0.0063.
Values may be sent and summed in bfloat16 or wider, within the bound.
No kernel may reach another device: no remote copies, remote signals or barrier semaphores. Data moves between devices by JAX's collectives and lax.ppermute only.
A program may use at most 128 MiB of HBM per device.

v0:
```python
import jax
import jax.numpy as jnp
from jax import lax
from jax.sharding import PartitionSpec as P

NB = 512
PANELS = 2


ATOM_RIDGE = 0.02
NORM_EPS = 1e-06


def from_root(block, axis, source):
    block = jnp.where(lax.axis_index(axis) == source, block, jnp.zeros_like(block))
    return lax.psum(block, axis)


def same_block(blocks):
    return blocks


def outgoing(unit_rows, kernel_slot, block_owner, per_device, capacity, devices):
    target = block_owner(kernel_slot // per_device)
    positions = jnp.arange(per_device, dtype=jnp.int32)
    earlier = (target[:, None] == target[None, :]) & (positions[None, :] < positions[:, None])
    rank_within = jnp.sum(earlier.astype(jnp.int32), axis=1)
    source_rows = (
        jnp.zeros((devices * capacity,), jnp.int32)
        .at[target * capacity + rank_within]
        .set(positions)
    )
    return jnp.take(unit_rows, source_rows, axis=0)


def incoming(received, slot_all, own_index, block_owner, per_device, capacity, devices):
    slot_table = slot_all.reshape(devices, per_device)
    arrives_here = block_owner(slot_table // per_device) == own_index
    rank_within = jnp.cumsum(arrives_here.astype(jnp.int32), axis=1) - 1
    sources = jnp.arange(devices, dtype=jnp.int32)[:, None]
    buffer_rows = sources * capacity + rank_within
    landing = jnp.where(arrives_here, slot_table % per_device, per_device)
    pick_rows = (
        jnp.zeros((per_device,), jnp.int32)
        .at[landing.reshape(-1)]
        .set(buffer_rows.reshape(-1), mode="drop")
    )
    return jnp.take(received, pick_rows, axis=0)


def body(spectra, projection, kernel_slot, env_image, image_atoms):
    grid_rows = lax.axis_size("row")
    grid_cols = lax.axis_size("col")
    devices = grid_rows * grid_cols
    per_device = spectra.shape[0]
    total_rows = per_device * devices
    reduced_width = projection.shape[1]
    row_group = total_rows // grid_rows
    col_group = total_rows // grid_cols
    capacity = max(1, per_device // devices)
    row_index = lax.axis_index("row")
    col_index = lax.axis_index("col")
    own_index = row_index * grid_cols + col_index
    projected = jnp.dot(spectra, projection, preferred_element_type=jnp.float32)
    factor = lax.rsqrt(
        jnp.mean(projected * projected, axis=1, keepdims=True) + NORM_EPS
    ) * reduced_width ** (-0.5)
    unit_rows = (projected * factor).astype(jnp.bfloat16)
    slot_all, image_all = (
        lax.all_gather(kernel_slot, ("row", "col"), axis=0, tiled=True),
        lax.all_gather(env_image, ("row", "col"), axis=0, tiled=True),
    )
    sent_rows = outgoing(unit_rows, kernel_slot, same_block, per_device, capacity, devices)
    received_rows = lax.all_to_all(
        sent_rows, ("row", "col"), split_axis=0, concat_axis=0, tiled=True
    )
    own_rows = incoming(
        received_rows, slot_all, own_index, same_block, per_device, capacity, devices
    )
    row_group_rows = lax.all_gather(own_rows, "col", axis=0, tiled=True)
    group_list = []
    for copy_index in range(grid_rows // grid_cols):
        group_list.append(from_root(row_group_rows, "row", col_index + copy_index * grid_cols))
    col_group_rows = jnp.concatenate(group_list, axis=0)
    gram_matrix = lax.dot_general(
        row_group_rows, col_group_rows, (((1,), (1,)), ((), ())), preferred_element_type=jnp.float32
    )
    inverse = (
        jnp.zeros((total_rows,), jnp.int32)
        .at[slot_all]
        .set(jnp.arange(total_rows, dtype=jnp.int32))
    )
    env_rows = lax.dynamic_slice_in_dim(inverse, row_index * row_group, row_group)
    image_rows = jnp.take(image_all, env_rows)
    image_count = image_atoms.shape[0]
    atom_count = jnp.sum(
        jnp.where(
            image_rows[:, None] == jnp.arange(image_count, dtype=jnp.int32)[None, :],
            image_atoms[None, :],
            0,
        ),
        axis=1,
    )
    ridge_diag = ATOM_RIDGE * atom_count.astype(jnp.float32)
    offset = row_index // grid_cols * row_group
    holds_diagonal = col_index == row_index % grid_cols
    row_positions = jnp.arange(row_group, dtype=jnp.int32)
    col_positions = jnp.arange(col_group, dtype=jnp.int32)
    diagonal_hit = (col_positions[None, :] == offset + row_positions[:, None]) & holds_diagonal
    covariance = gram_matrix * gram_matrix + jnp.where(diagonal_hit, ridge_diag[:, None], 0.0)
    row_tile = row_positions // NB * grid_rows + row_index
    panel_list = []
    for panel_index in range(PANELS):
        root_row = panel_index % grid_rows
        root_col = panel_index % grid_cols
        row_start = panel_index // grid_rows * NB
        col_start = root_row // grid_cols * row_group + row_start
        corner = lax.slice(covariance, (row_start, col_start), (row_start + NB, col_start + NB))
        pivot_tile = from_root(corner, "row", root_row)
        lower_factor = jnp.linalg.cholesky(pivot_tile)
        column = lax.slice_in_dim(covariance, col_start, col_start + NB, axis=1)
        solved = lax.linalg.triangular_solve(
            lower_factor, column, left_side=False, lower=True, transpose_a=True
        )
        solved = jnp.where((row_tile >= panel_index)[:, None], solved, 0.0)
        panel_row = from_root(solved, "col", root_col)
        copies = []
        for copy_index in range(grid_rows // grid_cols):
            copies.append(from_root(panel_row, "row", col_index + copy_index * grid_cols))
        panel_cols = jnp.concatenate(copies, axis=0)
        update = lax.dot_general(
            panel_row,
            panel_cols,
            (((1,), (1,)), ((), ())),
            precision=lax.Precision.HIGHEST,
            preferred_element_type=jnp.float32,
        )
        covariance = covariance - update
        panel_list.append(panel_row)
    panels = jnp.concatenate(panel_list, axis=1)
    return (panels, covariance)


def solution(mesh):
    in_specs = (P(("row", "col"), None), P(), P(("row", "col")), P(("row", "col")), P())
    out_specs = (P("row", None), P("row", "col"))
    return jax.shard_map(body, mesh=mesh, in_specs=in_specs, out_specs=out_specs, check_vma=False)
```

profile of v0, /device:TPU:1, one launch (start us, length us, event | category | flops | bytes accessed | tf_op | source)
XLA Modules:
  0.0 1150.6 jit_solution(3452723511936852365)
XLA Ops:
  7.9 34.4 %all-gather = s32[128,1,128]{2,1,0:T(1,128)S(1)} all-gather(s32[1,1,128]{2,1,0:T(1,128)} %bitcast.141), channel_id=1, replica_groups=mesh['row'=16,'col'=8] {'row','col'}, dimensions={0}, use_global_device_ids=true | all-gather | bytes 66048 | tf_op jit(solution)/shard_map/all_gather | solution.py:70
  44.7 60.3 %scatter_custom_fusion.1 = s32[128]{0:T(128)S(1)} fusion(s32[16384]{0:T(1024)S(1)} %get-tuple-element.84, s32[16384]{0:T(1024)S(1)} %bitcast.140, s32[]{:T(128)} %copy.130), kind=kCustom, calls=%fused_computation.223 | custom fusion | bytes 516 | tf_op jit(solution)/shard_map/scatter | solution.py:46
  132.8 22.2 %all-gather.4.cloned.1.call-done = bf16[1024,1024]{1,0:T(8,128)(2,1)} async-done(((bf16[128,1024]{1,0:T(8,128)(2,1)}), bf16[1024,1024]{1,0:T(8,128)(2,1)}) %all-gather.4.cloned.1.call-update) | async-done | bytes 2097168 | tf_op jit(solution)/shard_map/all_gather | solution.py:80
  159.0 60.3 %scatter_custom_fusion.2 = s32[16384]{0:T(1024)S(1)} fusion(s32[16384]{0:T(1024)S(1)} %get-tuple-element.83, s32[16384]{0:T(1024)S(1)} %iota.95, s32[]{:T(128)} %copy.130), kind=kCustom, calls=%fused_computation.176 | custom fusion | bytes 65540 | tf_op jit(solution)/shard_map/scatter | solution.py:91
  219.4 31.0 %all-gather.1 = s32[128,1,128]{2,1,0:T(1,128)S(1)} all-gather(s32[1,1,128]{2,1,0:T(1,128)S(1)} %bitcast.142), channel_id=1, replica_groups=mesh['row'=16,'col'=8] {'row','col'}, dimensions={0}, use_global_device_ids=true | all-gather | bytes 66048 | tf_op jit(solution)/shard_map/all_gather | solution.py:71
  274.6 85.4 %all-reduce.12.cloned.1.call-done = f32[512,512]{0,1:T(8,128)} async-done(((f32[512,512]{0,1:T(8,128)}), f32[512,512]{0,1:T(8,128)}) %all-reduce.12.cloned.1.call-update) | async-done | bytes 1048592 | tf_op jit(solution)/shard_map/psum | solution.py:16
  361.9 11.7 %cholesky.286 = f32[128,128]{1,0:T(8,128)S(1)} custom-call(f32[128,128]{1,0:T(8,128)S(1)} %cholesky.426), custom_call_target="Cholesky" | custom-call | tf_op jit(solution)/shard_map/jit(cholesky)/cholesky | solution.py:120
  384.3 11.7 %cholesky.305 = f32[128,128]{1,0:T(8,128)S(1)} custom-call(f32[128,128]{1,0:T(8,128)S(1)} %cholesky.430), custom_call_target="Cholesky" | custom-call | tf_op jit(solution)/shard_map/jit(cholesky)/cholesky | solution.py:120
  408.0 11.7 %cholesky.326 = f32[128,128]{1,0:T(8,128)S(1)} custom-call(f32[128,128]{1,0:T(8,128)S(1)} %cholesky.435), custom_call_target="Cholesky" | custom-call | tf_op jit(solution)/shard_map/jit(cholesky)/cholesky | solution.py:120
  430.8 11.7 %cholesky.343 = f32[128,128]{1,0:T(8,128)S(1)} custom-call(f32[128,128]{1,0:T(8,128)S(1)} %convolution_subtract_fusion.9), custom_call_target="Cholesky" | custom-call | tf_op jit(solution)/shard_map/jit(cholesky)/cholesky | solution.py:120
  454.6 39.3 %custom-call.30 = f32[4,128,128]{1,2,0:T(8,128)S(1)} custom-call(f32[4,128,128]{2,1,0:T(8,128)S(1)} %get-tuple-element.19), custom_call_target="InvertDiagBlocksLowerTriangular" | custom-call | tf_op jit(solution)/shard_map/triangular_solve/custom-call.3 | solution.py:122
  504.8 64.9 %all-reduce.14.cloned.1.call-done = f32[1024,512]{0,1:T(8,128)} async-done(((f32[1024,512]{0,1:T(8,128)}), f32[1024,512]{0,1:T(8,128)}) %all-reduce.14.cloned.1.call-update) | async-done | bytes 2097168 | tf_op jit(solution)/shard_map/psum | solution.py:16
  574.2 104.4 %all-reduce.22.cloned.1.call-done = (f32[1024,512]{0,1:T(8,128)}, f32[1024,512]{0,1:T(8,128)}) async-done(((f32[1024,512]{0,1:T(8,128)}, f32[1024,512]{0,1:T(8,128)}), (f32[1024,512]{0,1:T(8,128)}, f32[1024,512]{0,1:T(8,128)})) %all-reduce.22.cloned.1.call-update) | async-done | bytes 4194320 | tf_op jit(solution)/shard_map/psum | solution.py:16
  678.6 16.4 %fusion.15 = f32[1024,2048]{0,1:T(8,128)S(1)} fusion(f32[1024,2048]{0,1:T(8,128)} %copy-done.3, f32[1024,512]{0,1:T(8,128)S(1)} %copy-done.4, f32[1024,512]{0,1:T(8,128)} %get-tuple-element.49, f32[1024,512]{0,1:T(8,128)} %get-tuple-element.50), kind=kOutput, calls=%fused_computation.28 | convolution fusion | flops 12888047616 | bytes 23068672 | tf_op jit(solution)/shard_map/dot_general | solution.py:131
  700.1 85.4 %all-reduce.16.cloned.1.call-done = f32[512,512]{0,1:T(8,128)} async-done(((f32[512,512]{0,1:T(8,128)}), f32[512,512]{0,1:T(8,128)}) %all-reduce.16.cloned.1.call-update) | async-done | bytes 1048592 | tf_op jit(solution)/shard_map/psum | solution.py:16
  790.6 11.7 %cholesky.358 = f32[128,128]{1,0:T(8,128)S(1)} custom-call(f32[128,128]{1,0:T(8,128)S(1)} %cholesky.439), custom_call_target="Cholesky" | custom-call | tf_op jit(solution)/shard_map/jit(cholesky)/cholesky | solution.py:120
  814.8 11.7 %cholesky.377 = f32[128,128]{1,0:T(8,128)S(1)} custom-call(f32[128,128]{1,0:T(8,128)S(1)} %cholesky.443), custom_call_target="Cholesky" | custom-call | tf_op jit(solution)/shard_map/jit(cholesky)/cholesky | solution.py:120
  839.4 11.7 %cholesky.398 = f32[128,128]{1,0:T(8,128)S(1)} custom-call(f32[128,128]{1,0:T(8,128)S(1)} %cholesky.448), custom_call_target="Cholesky" | custom-call | tf_op jit(solution)/shard_map/jit(cholesky)/cholesky | solution.py:120
  863.1 11.7 %cholesky.415 = f32[128,128]{1,0:T(8,128)S(1)} custom-call(f32[128,128]{1,0:T(8,128)S(1)} %convolution_subtract_fusion.8), custom_call_target="Cholesky" | custom-call | tf_op jit(solution)/shard_map/jit(cholesky)/cholesky | solution.py:120
  879.3 11.7 %while.5 = (s32[]{:T(128)}, f32[512,512]{1,0:T(8,128)}, s32[4,2]{0,1:T(2,128)S(1)}, f32[4,128,128]{2,1,0:T(8,128)S(1)}, s32[]{:T(128)}) while((s32[]{:T(128)}, f32[512,512]{1,0:T(8,128)}, s32[4,2]{0,1:T(2,128)S(1)}, f32[4,128,128]{2,1,0:T(8,128)S(1)}, s32[]{:T(128)}) %tuple.91), condition=%wide.while_cond.clone, body=%wide.while_body.clone.sunk | while | flops 2 | bytes 131181 | solution.py:122
  891.0 39.3 %custom-call.34 = f32[4,128,128]{1,2,0:T(8,128)S(1)} custom-call(f32[4,128,128]{2,1,0:T(8,128)S(1)} %get-tuple-element.20), custom_call_target="InvertDiagBlocksLowerTriangular" | custom-call | tf_op jit(solution)/shard_map/triangular_solve/custom-call.3 | solution.py:122
  941.8 64.7 %all-reduce.18.cloned.1.call-done = f32[1024,512]{0,1:T(8,128)} async-done(((f32[1024,512]{0,1:T(8,128)}), f32[1024,512]{0,1:T(8,128)}) %all-reduce.18.cloned.1.call-update) | async-done | bytes 2097168 | tf_op jit(solution)/shard_map/psum | solution.py:16
  1020.4 94.9 %all-reduce.20.cloned.1.call-done = (f32[1024,512]{0,1:T(8,128)}, f32[1024,512]{0,1:T(8,128)}) async-done(((f32[1024,512]{0,1:T(8,128)}, f32[1024,512]{0,1:T(8,128)}), (f32[1024,512]{0,1:T(8,128)}, f32[1024,512]{0,1:T(8,128)})) %all-reduce.20.cloned.1.call-update) | async-done | bytes 4194320 | tf_op jit(solution)/shard_map/psum | solution.py:16
  1115.3 18.8 %fusion.12 = f32[1024,2048]{0,1:T(8,128)} fusion(f32[1024,2048]{0,1:T(8,128)} %copy-done.2, f32[1024,512]{0,1:T(8,128)S(1)} %copy-done.5, f32[1024,512]{0,1:T(8,128)} %get-tuple-element.47, f32[1024,512]{0,1:T(8,128)} %get-tuple-element.48), kind=kOutput, calls=%fused_computation.27 | convolution fusion | flops 12888047616 | bytes 23068672 | tf_op jit(solution)/shard_map/dot_general | solution.py:131
  (182 shorter events, 222.9 us)
Async XLA Ops:
  7.2 97.9 %copy-start = (bf16[128,4096]{1,0:T(8,128)(2,1)S(1)}, bf16[128,4096]{1,0:T(8,128)(2,1)}, u32[]{:S(2)}) copy-start(bf16[128,4096]{1,0:T(8,128)(2,1)} %param.10) | copy-start | bytes 3145732
  113.1 17.7 %all-to-all-start = ((bf16[128,2,512]{2,1,0:T(2,128)(2,1)}), bf16[128,2,512]{2,1,0:T(2,128)(2,1)S(1)}, u32[]{:S(2)}, u32[]{:S(2)}) async-start(bf16[128,2,512]{2,1,0:T(2,128)(2,1)} %reshape.208), calls=%async_computation | async-start | bytes 524288 | tf_op jit(solution)/shard_map/all_to_all | solution.py:74
  119.8 35.2 %all-gather.4.cloned.1.call-start = ((), (), s32[]{:S(2)}) async-start(), calls=%async_computation.1 | async-start | bytes 2359296 | tf_op jit(solution)/shard_map/all_gather | solution.py:80
  132.7 129.2 %all-reduce.24.cloned.1.call-start = ((), (), s32[]{:S(2)}) async-start(), calls=%async_computation.8 | async-start | bytes 8388608 | tf_op jit(solution)/shard_map/psum | solution.py:16
  158.9 60.5 %copy-start.11 = (s32[128]{0:T(128)S(1)}, s32[128]{0:T(128)}, u32[]{:S(2)}) copy-start(s32[128]{0:T(128)} %param.13) | copy-start | bytes 1540
  158.9 201.1 %all-reduce.12.cloned.1.call-start = ((), (), s32[]{:S(2)}) async-start(), calls=%async_computation.2 | async-start | bytes 2097152 | tf_op jit(solution)/shard_map/psum | solution.py:16
  250.4 6.2 copy-start.10
  250.4 11.5 copy-start.9
  269.6 3.4 copy-start.3
  274.1 295.7 %all-reduce.14.cloned.1.call-start = ((), (), s32[]{:S(2)}) async-start(), calls=%async_computation.3 | async-start | bytes 4194304 | tf_op jit(solution)/shard_map/psum | solution.py:16
  360.0 1.7 copy-start.6
  504.8 173.8 %all-reduce.22.cloned.1.call-start = ((), (), s32[]{:S(2)}) async-start(), calls=%async_computation.7 | async-start | bytes 8388608 | tf_op jit(solution)/shard_map/psum | solution.py:16
  574.1 104.5 %copy-start.4 = (f32[1024,512]{0,1:T(8,128)S(1)}, f32[1024,512]{0,1:T(8,128)}, u32[]{:S(2)}) copy-start(f32[1024,512]{0,1:T(8,128)} %all-reduce.14.cloned.1.call-done) | copy-start | bytes 6291460
  574.1 211.4 %all-reduce.16.cloned.1.call-start = ((), (), s32[]{:S(2)}) async-start(), calls=%async_computation.4 | async-start | bytes 2097152 | tf_op jit(solution)/shard_map/psum | solution.py:16
  695.1 3.4 copy-start.2
  699.6 306.9 %all-reduce.18.cloned.1.call-start = ((), (), s32[]{:S(2)}) async-start(), calls=%async_computation.5 | async-start | bytes 4194304 | tf_op jit(solution)/shard_map/psum | solution.py:16
  785.5 2.6 copy-start.7
  789.6 1.0 copy-start.8
  941.5 173.9 %all-reduce.20.cloned.1.call-start = ((), (), s32[]{:S(2)}) async-start(), calls=%async_computation.6 | async-start | bytes 8388608 | tf_op jit(solution)/shard_map/psum | solution.py:16
  1014.9 100.4 %copy-start.5 = (f32[1024,512]{0,1:T(8,128)S(1)}, f32[1024,512]{0,1:T(8,128)}, u32[]{:S(2)}) copy-start(f32[1024,512]{0,1:T(8,128)} %all-reduce.18.cloned.1.call-done) | copy-start | bytes 6291460
  1134.1 9.2 copy-start.1
Sparse Core Ops, SparseCore 0:
  132.8 22.1 all-gather.3
  159.0 102.8 all-reduce.23
  274.2 85.7 all-reduce.11
  504.9 64.8 all-reduce.13
  574.2 104.3 all-reduce.21
  699.7 85.7 all-reduce.15
  941.6 64.7 all-reduce.17
  1011.0 104.3 all-reduce.19
where the time goes:
time: 1160 us; the launch traced here: 1150 us
  waiting for transfers between devices  537 us (46%)
  other arithmetic  267 us (23%)
  local copies, waits for them, and re-layouts  178 us (15%)
  matrix products  73.4 us (6%)
  blocking collectives  65.4 us (6%)
  between operations  20.4 us (2%)
    psum x7, waiting for transfers between devices, from_root(): return lax.psum(block, axis)  504 us
    another operation x30, other arithmetic, body(): lower_factor = jnp.linalg.cholesky(pivot_tile)  158 us
    another operation x5, other arithmetic, body(): lax.linalg.triangular_solve(lower_factor, column, left_side=False, lower=...  80.3 us
    scatter x1, local copies, waits for them, and re-layouts, body(): inverse = jnp.zeros((total_rows,), jnp.int32).at[slot_all].set(jnp.arange...  60.3 us
    scatter x1, local copies, waits for them, and re-layouts, incoming(): pick_rows = jnp.zeros((per_device,), jnp.int32).at[landing.reshape(-1)].s...  60.3 us
    dot_general x2, matrix products, body(): lax.dot_general(panel_row, panel_cols, (((1,), (1,)), ((), ())), precisio...  35.2 us
    all_gather x1, blocking collectives, body(): lax.all_gather(kernel_slot, ('row', 'col'), axis=0, tiled=True)  34.4 us
    all_gather x1, blocking collectives, body(): lax.all_gather(env_image, ('row', 'col'), axis=0, tiled=True)  31 us
  transfers between devices with their start and end apart: 9, of which 9 were waited for; matrix products, arithmetic and copies ran while one was open for 7% of the time, Pallas kernels for 0%

commit v1 on v0

v1 whole, which is shorter than its diff:
```python
import functools

import jax
import jax.numpy as jnp
from jax import lax
from jax.experimental import pallas as pl
from jax.experimental.pallas import tpu as pltpu
from jax.sharding import PartitionSpec as P

NB = 512
PANELS = 2
ATOM_RIDGE = 0.02
NORM_EPS = 1e-06
EXTRA = 128
BLOCK = 128
NN = ((1,), (0,))
NT = ((1,), (1,))


def split(a):
    high = a.astype(jnp.bfloat16)
    return high, (a - high.astype(jnp.float32)).astype(jnp.bfloat16)


def halves(a):
    high = lax.reduce_precision(a, 8, 7)
    return high.astype(jnp.bfloat16), (a - high).astype(jnp.bfloat16)


def dot(a, b, dims):
    return lax.dot_general(a, b, (dims, ((), ())), preferred_element_type=jnp.float32)


def dot3(a, b, dims):
    a_high, a_low = a
    b_high, b_low = b
    return dot(a_high, b_high, dims) + (dot(a_high, b_low, dims) + dot(a_low, b_high, dims))


def eliminate(rows, lane, sub):
    mat = list(rows)
    count = len(mat)
    inv = [jnp.where(lane == sub + 8 * i, 1.0, 0.0).astype(jnp.float32) for i in range(count)]
    out = [None] * count

    def wide(value):
        return jnp.broadcast_to(value, (8, BLOCK))

    for j in range(0, 8 * count, 2):
        v, s = j // 8, j % 8
        row0, row1 = wide(mat[v][s : s + 1, :]), wide(mat[v][s + 1 : s + 2, :])
        inv0, inv1 = wide(inv[v][s : s + 1, :]), wide(inv[v][s + 1 : s + 2, :])
        a, b, c = wide(row0[:, j : j + 1]), wide(row0[:, j + 1 : j + 2]), wide(row1[:, j + 1 : j + 2])
        det = a * c - b * b
        r = 1.0 / det
        p0, p1 = (c * row0 - b * row1) * r, (a * row1 - b * row0) * r
        q0, q1 = (c * inv0 - b * inv1) * r, (a * inv1 - b * inv0) * r
        ra, rd = lax.rsqrt(a), lax.rsqrt(det)
        done0, done1 = inv0 * ra, (a * inv1 - b * inv0) * (ra * rd)
        before = inv[v] if out[v] is None else out[v]
        out[v] = jnp.where(sub == s, done0, jnp.where(sub == s + 1, done1, before))
        for i in range(v, count):
            if i == v and s == 6:
                continue
            c0, c1 = wide(mat[i][:, j : j + 1]), wide(mat[i][:, j + 1 : j + 2])
            if i == v:
                keep = sub > s + 1
                c0, c1 = jnp.where(keep, c0, 0.0), jnp.where(keep, c1, 0.0)
            mat[i] = mat[i] - (c0 * p0 + c1 * p1)
            inv[i] = inv[i] - (c0 * q0 + c1 * q1)
    return out


def inverse_factor_kernel(n, a_ref, x_ref, w_ref, d_ref):
    lane = lax.broadcasted_iota(jnp.int32, (8, BLOCK), 1)
    sub = lax.broadcasted_iota(jnp.int32, (8, BLOCK), 0)
    w_ref[:, :n] = a_ref[...]
    diagonal = lax.broadcasted_iota(jnp.int32, (n, n), 0) == lax.broadcasted_iota(jnp.int32, (n, n), 1)
    w_ref[:, n:] = jnp.where(diagonal, 1.0, 0.0)

    def step(k, carry):
        at = pl.multiple_of(k * BLOCK, BLOCK)
        corner = w_ref[pl.ds(at, BLOCK), pl.ds(at, BLOCK)]
        rows = eliminate([corner[8 * i : 8 * i + 8, :] for i in range(BLOCK // 8)], lane, sub)
        for i in range(BLOCK // 8):
            d_ref[8 * i : 8 * i + 8, :] = rows[i]
        inv = split(d_ref[...])
        upper = dot3(inv, split(w_ref[pl.ds(at, BLOCK), :]), NN)
        x_ref[pl.ds(at, BLOCK), :] = upper[:, n:]
        upper = split(upper)

        def update(i, carry):
            here = pl.multiple_of(i * BLOCK, BLOCK)
            lower = dot3(split(w_ref[pl.ds(here, BLOCK), pl.ds(at, BLOCK)]), inv, NT)
            w_ref[pl.ds(here, BLOCK), :] = w_ref[pl.ds(here, BLOCK), :] - dot3(split(lower), upper, NN)
            return carry

        lax.fori_loop(k + 1, n // BLOCK, update, 0)
        return carry

    lax.fori_loop(0, n // BLOCK, step, 0)


def inverse_factor(a):
    n = a.shape[0]
    return pl.pallas_call(
        functools.partial(inverse_factor_kernel, n),
        out_shape=jax.ShapeDtypeStruct((n, n), jnp.float32),
        in_specs=[pl.BlockSpec(memory_space=pltpu.VMEM)],
        out_specs=pl.BlockSpec(memory_space=pltpu.VMEM),
        scratch_shapes=[pltpu.VMEM((n, 2 * n), jnp.float32), pltpu.VMEM((BLOCK, BLOCK), jnp.float32)],
        compiler_params=pltpu.CompilerParams(vmem_limit_bytes=40 << 20),
        name="inverse_factor",
    )(a)


def in_block_order(rows):
    place = rows[:, -EXTRA].astype(jnp.int32)
    pick = lax.broadcasted_iota(jnp.int32, (rows.shape[0], rows.shape[0]), 0) == place[None, :]
    return dot(pick.astype(jnp.bfloat16), rows, NN).astype(jnp.bfloat16)


def body(spectra, projection, kernel_slot, env_image, image_atoms):
    grid_rows = lax.axis_size("row")
    grid_cols = lax.axis_size("col")
    devices = grid_rows * grid_cols
    per_device = spectra.shape[0]
    total_rows = per_device * devices
    width = projection.shape[1]
    row_group = total_rows // grid_rows
    col_group = total_rows // grid_cols
    row_index = lax.axis_index("row")
    col_index = lax.axis_index("col")
    projected = jnp.dot(spectra, projection, preferred_element_type=jnp.float32)
    factor = lax.rsqrt(
        jnp.mean(projected * projected, axis=1, keepdims=True) + NORM_EPS
    ) * width ** (-0.5)
    unit_rows = (projected * factor).astype(jnp.bfloat16)

    images = jnp.arange(image_atoms.shape[0], dtype=jnp.int32)
    atoms = jnp.sum(jnp.where(env_image[:, None] == images[None, :], image_atoms[None, :], 0), axis=1)
    extra_lane = jnp.arange(EXTRA, dtype=jnp.int32)[None, :]
    extra = jnp.where(extra_lane == 0, (kernel_slot % per_device)[:, None], atoms[:, None])
    packed = jnp.concatenate([unit_rows, extra.astype(jnp.bfloat16)], axis=1)

    block = kernel_slot // per_device
    blocks = jnp.arange(devices, dtype=jnp.int32)
    by_block = dot((blocks[:, None] == block[None, :]).astype(jnp.bfloat16), packed, NN).astype(jnp.bfloat16)
    dest_row, dest_col = blocks // grid_cols, blocks % grid_cols
    turned_block = (dest_col + grid_cols * (dest_row // grid_cols)) * grid_cols + dest_row % grid_cols
    by_turned = dot((turned_block[:, None] == block[None, :]).astype(jnp.bfloat16), packed, NN).astype(jnp.bfloat16)

    tile_blocks = NB // per_device
    group_blocks = row_group // per_device
    pivot_rows = []
    for panel_index in range(PANELS):
        first = panel_index % grid_rows * group_blocks + panel_index // grid_rows * tile_blocks
        pivot_rows.append(by_block[first : first + tile_blocks])
    pivot_rows = jnp.concatenate(pivot_rows, axis=0)
    pivot_blocks = pivot_rows.shape[0]
    spread = jnp.broadcast_to(pivot_rows[None], (devices,) + pivot_rows.shape)

    both = ("row", "col")
    pivots = lax.all_to_all(spread, both, split_axis=0, concat_axis=0, tiled=True)
    turned = lax.all_to_all(by_turned, both, split_axis=0, concat_axis=0, tiled=True)
    own = lax.all_to_all(by_block, both, split_axis=0, concat_axis=0, tiled=True)
    col_rows = lax.all_gather(in_block_order(turned)[:, :width], "row", axis=0, tiled=True)
    row_rows = lax.all_gather(in_block_order(own), "col", axis=0, tiled=True)

    pivots = jnp.concatenate([in_block_order(pivots[:, i]) for i in range(pivot_blocks)], axis=0)
    order = pivots.shape[0]
    pivot_ridge = ATOM_RIDGE * pivots[:, -1].astype(jnp.float32)
    pivots = pivots[:, :width]
    pivot_gram = dot(pivots, pivots, NT)
    diagonal = jnp.arange(order)[:, None] == jnp.arange(order)[None, :]
    inverse = inverse_factor(pivot_gram * pivot_gram + jnp.where(diagonal, pivot_ridge[:, None], 0.0))

    ridge = ATOM_RIDGE * row_rows[:, -1].astype(jnp.float32)
    row_rows = row_rows[:, :width]
    positions = jnp.arange(row_group, dtype=jnp.int32)
    row_tile = positions // NB * grid_rows + row_index
    pivot_of = jnp.arange(order, dtype=jnp.int32)
    pivot_stored = pivot_of // NB % grid_rows * row_group + pivot_of // NB // grid_rows * NB + pivot_of % NB
    stored = row_index * row_group + positions
    row_gram = dot(row_rows, pivots, NT)
    row_cov = row_gram * row_gram + jnp.where(stored[:, None] == pivot_stored[None, :], ridge[:, None], 0.0)
    inverse_parts = halves(inverse)
    panels = dot3(halves(row_cov), inverse_parts, NT)
    panels = jnp.where(row_tile[:, None] >= pivot_of[None, :] // NB, panels, 0.0)
    weights = dot3(halves(panels), inverse_parts, NN)

    col_gram = dot(pivots, col_rows, NT)
    groups = jnp.arange(col_group, dtype=jnp.int32) // row_group * grid_cols + col_index
    col_stored = groups * row_group + jnp.arange(col_group, dtype=jnp.int32) % row_group
    col_hit = pivot_stored[:, None] == col_stored[None, :]
    col_cov = col_gram * col_gram + jnp.where(col_hit, pivot_ridge[:, None], 0.0)
    gram = dot(row_rows, col_rows, NT)
    covariance = gram * gram + jnp.where(stored[:, None] == col_stored[None, :], ridge[:, None], 0.0)
    trailing = covariance - dot3(halves(weights), halves(col_cov), NN)
    return panels, trailing


def solution(mesh):
    in_specs = (P(("row", "col"), None), P(), P(("row", "col")), P(("row", "col")), P())
    out_specs = (P("row", None), P("row", "col"))
    return jax.shard_map(body, mesh=mesh, in_specs=in_specs, out_specs=out_specs, check_vma=False)
```

time: 1160 us -> 302 us (0.26)
  waiting for transfers between devices: 537 us -> 46.3 us
  other arithmetic: 267 us -> 6.65 us
  local copies, waits for them, and re-layouts: 178 us -> 12 us
  Pallas kernels: 0 us -> 98.5 us
  blocking collectives: 65.4 us -> 22.8 us
  matrix products: 73.4 us -> 86.2 us
    psum x7 -> x0, waiting for transfers between devices: 504 us -> none  [from_root(): return lax.psum(block, axis)]
    another operation x36 -> x0, other arithmetic: 239 us -> none  [the longest x30 158 us: body(): lower_factor = jnp.linalg.cholesky(pivot_tile)]
    scatter x3 -> x0, local copies, waits for them, and re-layouts: 122 us -> none  [the longest x1 60.3 us: body(): inverse = jnp.zeros((total_rows,), jnp.int32).at[slot_all].set(jnp.arange...]
    pallas_call x0 -> x1, Pallas kernels: none -> 98.5 us  [inverse_factor(): pl.pallas_call(functools.partial(inverse_factor_kernel, n), out_shape=jax...]
    all_gather x2 -> x0, blocking collectives: 65.4 us -> none  [the longest x1 34.4 us: body(): lax.all_gather(kernel_slot, ('row', 'col'), axis=0, tiled=True)]
    dot_general x3 -> x25, matrix products: 42.9 us -> 81.5 us  [dot(): lax.dot_general(a, b, (dims, ((), ())), preferred_element_type=jnp.float32)]
    all_to_all x1 -> x2, waiting for transfers between devices: 10.8 us -> 46.3 us  [the longest x1 34.7 us: body(): lax.all_to_all(spread, both, split_axis=0, concat_axis=0, tiled=True)]
    another operation x26 -> x0, matrix products: 25.8 us -> none  [the longest x14 18.5 us: body(): lax.linalg.triangular_solve(lower_factor, column, left_side=False, lower=...]
  transfers between devices with their start and end apart: 9 -> 4, of which waited for: 9 -> 2; matrix products, arithmetic and copies ran while one was open for 7% -> 16% of each run, Pallas kernels for 0% -> 33%
where the time goes in v1:
time: 302 us; the launch traced here: 297 us
  Pallas kernels  98.5 us (33%)
  matrix products  86.2 us (29%)
  waiting for transfers between devices  46.3 us (15%)
  blocking collectives  22.8 us (8%)
  between operations  14.6 us (5%)
  local copies, waits for them, and re-layouts  12 us (4%)
  starting transfers between devices  9.49 us (3%)
  other arithmetic  6.65 us (2%)
    pallas_call x1, Pallas kernels, inverse_factor(): pl.pallas_call(functools.partial(inverse_factor_kernel, n), out_shape=jax...  98.5 us
    dot_general x25, matrix products, dot(): lax.dot_general(a, b, (dims, ((), ())), preferred_element_type=jnp.float32)  81.5 us
    all_to_all x1, waiting for transfers between devices, body(): lax.all_to_all(spread, both, split_axis=0, concat_axis=0, tiled=True)  34.7 us
    all_to_all x1, blocking collectives, body(): lax.all_to_all(by_block, both, split_axis=0, concat_axis=0, tiled=True)  22.8 us
    all_to_all x1, waiting for transfers between devices, body(): lax.all_to_all(by_turned, both, split_axis=0, concat_axis=0, tiled=True)  11.6 us
  transfers between devices with their start and end apart: 4, of which 2 were waited for; matrix products, arithmetic and copies ran while one was open for 16% of the time, Pallas kernels for 33%

profile of v1, /device:TPU:1, one launch (start us, length us, event | category | flops | bytes accessed | tf_op | source)
XLA Modules:
  0.0 296.6 jit_solution(15750914975598619654)
XLA Ops:
  8.4 4.7 %multiply_reduce_fusion.2 = (f32[128]{0:T(128)S(1)}, f32[128,1024]{1,0:T(8,128)S(1)}) fusion(bf16[128,4096]{1,0:T(8,128)(2,1)S(1)} %copy-done, bf16[4096,1024]{1,0:T(8,128)(2,1)} %param.6), kind=kOutput, calls=%fused_computation.70 | convolution fusion | flops 1074003840 | bytes 9961984 | tf_op jit(solution)/shard_map/dot_general | solution.py:134
  15.5 22.8 %all_to_all.29 = bf16[128,2,576]{2,1,0:T(2,128)(2,1)S(1)} all-to-all(bf16[128,2,576]{2,1,0:T(2,128)(2,1)S(1)} %reshape.335), channel_id=1, replica_groups=mesh['row'=16,'col'=8] {'row','col'}, dimensions={0} | all-to-all | bytes 589824 | tf_op jit(solution)/shard_map/all_to_all | solution.py:166
  42.0 4.6 %all-to-all-start.2 = ((bf16[128,2,576]{2,1,0:T(2,128)(2,1)}), bf16[128,2,576]{2,1,0:T(2,128)(2,1)S(1)}, u32[]{:S(2)}, u32[]{:S(2)}) async-start(bf16[128,2,576]{2,1,0:T(2,128)(2,1)} %reshape.337), calls=%async_computation.2 | async-start | bytes 655360 | tf_op jit(solution)/shard_map/all_to_all | solution.py:165
  46.7 11.6 %all-to-all-done.2 = bf16[128,2,576]{2,1,0:T(2,128)(2,1)S(1)} async-done(((bf16[128,2,576]{2,1,0:T(2,128)(2,1)}), bf16[128,2,576]{2,1,0:T(2,128)(2,1)S(1)}, u32[]{:S(2)}, u32[]{:S(2)}) %all-to-all-start.2) | async-done | bytes 294944 | tf_op jit(solution)/shard_map/all_to_all | solution.py:165
  58.2 1.6 broadcast_in_dim.124
  59.8 4.7 %all-to-all-start.1 = ((bf16[128,8,1152]{2,1,0:T(8,128)(2,1)}), bf16[128,8,1152]{2,1,0:T(8,128)(2,1)S(1)}, u32[]{:S(2)}, u32[]{:S(2)}) async-start(bf16[128,8,1152]{2,1,0:T(8,128)(2,1)} %broadcast_in_dim.124), calls=%async_computation.1 | async-start | bytes 4718592 | tf_op jit(solution)/shard_map/all_to_all | solution.py:164
  66.4 34.7 %all-to-all-done.1 = bf16[128,8,1152]{2,1,0:T(8,128)(2,1)S(1)} async-done(((bf16[128,8,1152]{2,1,0:T(8,128)(2,1)}), bf16[128,8,1152]{2,1,0:T(8,128)(2,1)S(1)}, u32[]{:S(2)}, u32[]{:S(2)}) %all-to-all-start.1) | async-done | bytes 2359328 | tf_op jit(solution)/shard_map/all_to_all | solution.py:164
  101.1 3.9 %fusion.93 = (bf16[128,1,1152]{2,1,0:T(2,128)(2,1)S(1)}, bf16[128,1,1152]{2,1,0:T(2,128)(2,1)S(1)}, bf16[128,1,1152]{2,1,0:T(2,128)(2,1)S(1)}, bf16[128,1,1152]{...) fusion(bf16[128,8,1152]{2,1,0:T(8,128)(2,1)S(1)} %all-to-all-done.1), kind=kLoop, calls=%fused_computation.187 | loop fusion | bytes 4718592 | tf_op jit(solution)/shard_map/slice | solution.py:170
  113.9 1.2 multiply_reduce_fusion
  115.2 4.7 %select_add_fusion.1.a_ref = f32[1024,1024]{1,0:T(8,128)S(1)} fusion(f32[1024]{0:T(1024)S(1)} %multiply_reduce_fusion, bf16[1024,1152]{1,0:T(8,128)(2,1)} %fusion.11), kind=kOutput, calls=%fused_computation.23 | convolution fusion | flops 2151677952 | bytes 6295552 | tf_op jit(solution)/shard_map/dot_general | solution.py:31
  119.9 98.5 %inverse_factor.1 = f32[1024,1024]{1,0:T(8,128)S(1)} custom-call(f32[1024,1024]{1,0:T(8,128)S(1)} %select_add_fusion.1.a_ref), custom_call_target="tpu_custom_call" | custom-call | tf_op jit(solution)/shard_map/inverse_factor/pallas_call | solution.py:106
  218.4 2.0 copy-done.2
  222.0 4.6 %fusion.33 = f32[1024,1024]{1,0:T(8,128)S(1)} fusion(bf16[1024,1152]{1,0:T(8,128)(2,1)} %all-gather.3.cloned.1.call-done, bf16[1024,1152]{1,0:T(8,128)(2,1)} %fusion.11), kind=kOutput, calls=%fused_computation.55 | convolution fusion | flops 2147483648 | bytes 8388608 | tf_op jit(solution)/shard_map/dot_general | solution.py:31
  226.6 2.4 fusion.92
  229.0 2.4 fusion.42
  231.5 2.7 add_select_fusion
  234.2 2.4 fusion.39
  236.5 2.4 fusion.22
  238.9 4.8 %add_add_fusion = f32[1024,1024]{1,0:T(8,128)} fusion(f32[1024,1024]{1,0:T(8,128)S(1)} %fusion.39, f32[1024,1024]{1,0:T(8,128)S(1)} %fusion.22, f32[1024,1024]{1,0:T(8,128)S(1)} %add_select_fusion, f32[1024,1024]{1,0:T(8,128)S(1)} %copy-done.3), kind=kOutput, calls=%fused_computation.19 | convolution fusion | flops 2154823680 | bytes 20971520 | tf_op jit(solution)/shard_map/dot_general | solution.py:31
  243.7 7.2 %fusion.35 = f32[1024,2048]{1,0:T(8,128)S(1)} fusion(bf16[2048,1024]{1,0:T(8,128)(2,1)} %all-gather.5.cloned.1.call-done, bf16[1024,1152]{1,0:T(8,128)(2,1)} %fusion.11), kind=kOutput, calls=%fused_computation.57 | convolution fusion | flops 4294967296 | bytes 14680064 | tf_op jit(solution)/shard_map/dot_general | solution.py:31
  250.9 8.1 %fusion.20 = f32[1024,2048]{1,0:T(8,128)} fusion(f32[1024,1024]{1,0:T(8,128)S(1)} %copy-done.5, f32[1024,2048]{1,0:T(8,128)S(1)} %fusion.35, f32[1024]{0:T(1024)S(1)} %multiply_reduce_fusion, s32[2048]{0:T(1024)S(1)} %fusion.68, s32[1024]{0:T(1024)S(1)} %get-tuple-element.22), kind=kOutput, calls=%fused_computation.47 | convolution fusion | flops 4310695936 | bytes 20987904 | tf_op jit(solution)/shard_map/dot_general | solution.py:31
  259.0 7.0 %fusion.5 = f32[1024,2048]{1,0:T(8,128)} fusion(f32[1024,2048]{1,0:T(8,128)S(1)} %fusion.35, f32[1024]{0:T(1024)S(1)} %multiply_reduce_fusion, s32[2048]{0:T(1024)S(1)} %fusion.68, s32[1024]{0:T(1024)S(1)} %get-tuple-element.22, f32[1024,1024]{1,0:T(8,128)S(1)} %copy-done.5), kind=kOutput, calls=%fused_computation.17 | convolution fusion | flops 4311744512 | bytes 20987904 | tf_op jit(solution)/shard_map/dot_general | solution.py:31
  266.0 7.1 %fusion.40 = f32[1024,2048]{1,0:T(8,128)} fusion(f32[1024,1024]{1,0:T(8,128)S(1)} %copy-done.5, f32[1024,2048]{1,0:T(8,128)S(1)} %fusion.35, f32[1024]{0:T(1024)S(1)} %multiply_reduce_fusion, s32[2048]{0:T(1024)S(1)} %fusion.68, s32[1024]{0:T(1024)S(1)} %get-tuple-element.22), kind=kOutput, calls=%fused_computation.62 | convolution fusion | flops 4309647360 | bytes 20987904 | tf_op jit(solution)/shard_map/dot_general | solution.py:31
  273.1 16.5 %add_subtract_fusion = f32[1024,2048]{1,0:T(8,128)} fusion(f32[1024,2048]{1,0:T(8,128)} %fusion.40, f32[1024,2048]{1,0:T(8,128)} %fusion.5, f32[1024,2048]{1,0:T(8,128)} %fusion.20, bf16[2048,1024]{1,0:T(8,128)(2,1)} %all-gather.5.cloned.1.call-done, f32[1024]{0:T(1024)S(1)} %multiply_reduce_fusion.1, s32[2048]{0:T(1024)S(1)} %fusion.68, ...), kind=kOutput, calls=%fused_computation.3 | convolution fusion | flops 4309647360 | bytes 39862272 | tf_op jit(solution)/shard_map/dot_general | solution.py:31
  (74 shorter events, 19.5 us)
Async XLA Ops:
  7.2 1.2 copy-start
  7.2 213.5 %all-gather.3.cloned.1.call-start = ((), (), s32[]{:S(2)}) async-start(), calls=%async_computation.3 | async-start | bytes 2654208 | tf_op jit(solution)/shard_map/all_gather | solution.py:168
  8.4 4.8 %copy-start.7 = (s32[1024]{0:T(1024)S(1)}, s32[1024]{0:T(1024)}, u32[]{:S(2)}) copy-start(s32[1024]{0:T(1024)} %param.9) | copy-start | bytes 12292
  8.4 4.8 %copy-start.8 = (s32[128]{0:T(128)S(1)}, s32[128]{0:T(128)}, u32[]{:S(2)}) copy-start(s32[128]{0:T(128)} %param.8) | copy-start | bytes 1540
  42.0 16.2 %all-to-all-start.2 = ((bf16[128,2,576]{2,1,0:T(2,128)(2,1)}), bf16[128,2,576]{2,1,0:T(2,128)(2,1)S(1)}, u32[]{:S(2)}, u32[]{:S(2)}) async-start(bf16[128,2,576]{2,1,0:T(2,128)(2,1)} %reshape.337), calls=%async_computation.2 | async-start | bytes 655360 | tf_op jit(solution)/shard_map/all_to_all | solution.py:165
  59.8 41.3 %all-to-all-start.1 = ((bf16[128,8,1152]{2,1,0:T(8,128)(2,1)}), bf16[128,8,1152]{2,1,0:T(8,128)(2,1)S(1)}, u32[]{:S(2)}, u32[]{:S(2)}) async-start(bf16[128,8,1152]{2,1,0:T(8,128)(2,1)} %broadcast_in_dim.124), calls=%async_computation.1 | async-start | bytes 4718592 | tf_op jit(solution)/shard_map/all_to_all | solution.py:164
  64.5 179.3 %all-gather.5.cloned.1.call-start = ((), (), s32[]{:S(2)}) async-start(), calls=%async_computation.4 | async-start | bytes 4456448 | tf_op jit(solution)/shard_map/all_gather | solution.py:167
  218.3 2.0 copy-start.2
  226.6 2.5 copy-start.3
  234.2 4.7 %copy-start.4 = (f32[1024,1024]{1,0:T(8,128)}, f32[1024,1024]{1,0:T(8,128)S(1)}, u32[]{:S(2)}) copy-start(f32[1024,1024]{1,0:T(8,128)S(1)} %add_select_fusion) | copy-start | bytes 12582916
  243.7 7.2 %copy-start.5 = (f32[1024,1024]{1,0:T(8,128)S(1)}, f32[1024,1024]{1,0:T(8,128)}, u32[]{:S(2)}) copy-start(f32[1024,1024]{1,0:T(8,128)} %add_add_fusion) | copy-start | bytes 12582916
  266.0 7.1 %copy-start.6 = (bf16[1024,1152]{1,0:T(8,128)(2,1)S(1)}, bf16[1024,1152]{1,0:T(8,128)(2,1)}, u32[]{:S(2)}) copy-start(bf16[1024,1152]{1,0:T(8,128)(2,1)} %all-gather.3.cloned.1.call-done) | copy-start | bytes 7077892
  273.1 16.5 %copy-start.1 = (bf16[128,4096]{1,0:T(8,128)(2,1)S(1)}, bf16[128,4096]{1,0:T(8,128)(2,1)}, u32[]{:S(2)}) copy-start(bf16[128,4096]{1,0:T(8,128)(2,1)} %param.5) | copy-start | bytes 3145732
Sparse Core Ops, SparseCore 0:
  40.0 24.9 all-gather.2
  67.4 59.8 all-gather.4

commit v2 on v1

v2 whole, which is shorter than its diff:
```python
import functools

import jax
import jax.numpy as jnp
from jax import lax
from jax.experimental import pallas as pl
from jax.experimental.pallas import tpu as pltpu
from jax.sharding import PartitionSpec as P

NB = 512
PANELS = 2
ATOM_RIDGE = 0.02
NORM_EPS = 1e-06
EXTRA = 128
PIVOT_ATOMS = 1
OWN_ATOMS = 4
BLOCK = 128
NN = ((1,), (0,))
NT = ((1,), (1,))


def split(a):
    high = a.astype(jnp.bfloat16)
    return high, (a - high.astype(jnp.float32)).astype(jnp.bfloat16)


def halves(a):
    high = lax.reduce_precision(a, 8, 7)
    return high.astype(jnp.bfloat16), (a - high).astype(jnp.bfloat16)


def dot(a, b, dims):
    return lax.dot_general(a, b, (dims, ((), ())), preferred_element_type=jnp.float32)


def dot3(a, b, dims):
    a_high, a_low = a
    b_high, b_low = b
    return dot(a_high, b_high, dims) + (dot(a_high, b_low, dims) + dot(a_low, b_high, dims))


def eliminate(mat_ref, inv_ref, out_ref):
    sub = lax.broadcasted_iota(jnp.int32, (8, BLOCK), 0)
    column = lax.broadcasted_iota(jnp.int32, (8, BLOCK), 1)
    count = BLOCK // 8

    def wide(value):
        return jnp.broadcast_to(value, (8, BLOCK))

    for v in range(count):
        inv_ref[8 * v : 8 * v + 8, :] = jnp.where(column == sub + 8 * v, 1.0, 0.0)
    for v in range(count):
        mat, inv = mat_ref[8 * v : 8 * v + 8, :], inv_ref[8 * v : 8 * v + 8, :]
        cols = [wide(mat[:, 8 * v + k : 8 * v + k + 1]) for k in range(8)]
        done = inv
        for s in range(0, 8, 2):
            c0, c1 = cols[s], cols[s + 1]
            a, b, c = wide(c0[s : s + 1]), wide(c0[s + 1 : s + 2]), wide(c1[s + 1 : s + 2])
            det = a * c - b * b
            r = 1.0 / det
            ar, br, cr = a * r, b * r, c * r
            u, w = c0 * cr - c1 * br, c1 * ar - c0 * br
            u = jnp.where(sub == s, 1.0 - cr, jnp.where(sub == s + 1, br, u))
            w = jnp.where(sub == s, br, jnp.where(sub == s + 1, 1.0 - ar, w))

            def apply(x):
                return x - (u * wide(x[s : s + 1]) + w * wide(x[s + 1 : s + 2]))

            for k in range(s + 2, 8):
                cols[k] = apply(cols[k])
            i0, i1 = wide(inv[s : s + 1]), wide(inv[s + 1 : s + 2])
            ra = lax.rsqrt(a)
            done = jnp.where(sub == s, i0 * ra, jnp.where(sub == s + 1, (a * i1 - b * i0) * (ra * lax.rsqrt(det)), done))
            mat, inv = apply(mat), apply(inv)
        out_ref[8 * v : 8 * v + 8, :] = done
        mats = [wide(mat[k : k + 1]) for k in range(8)]
        invs = [wide(inv[k : k + 1]) for k in range(8)]
        for i in range(v + 1, count):
            at = slice(8 * i, 8 * i + 8)
            x = mat_ref[at, :]
            parts = [wide(x[:, 8 * v + k : 8 * v + k + 1]) for k in range(8)]
            mat_ref[at, :] = x - tree_sum([p * m for p, m in zip(parts, mats)])
            inv_ref[at, :] = inv_ref[at, :] - tree_sum([p * m for p, m in zip(parts, invs)])


def tree_sum(values):
    while len(values) > 1:
        values = [values[i] + values[i + 1] for i in range(0, len(values), 2)]
    return values[0]


def pivot_kernel(n, width, raw_ref, rows_ref, high_ref, low_ref, sorted_ref, w_ref, mat_ref, inv_ref, out_ref):
    k = pl.program_id(0)
    count = n // BLOCK

    @pl.when(k == 0)
    def _():
        raw = raw_ref[:, : width + EXTRA]
        pick = (lax.broadcasted_iota(jnp.int32, (8, EXTRA), 1) == 0).astype(jnp.bfloat16)
        place = dot(pick, raw[:, width:], NT)[0:1, :].astype(jnp.int32)
        target = lax.broadcasted_iota(jnp.int32, (1, n), 1) % count * BLOCK + place
        chosen = jnp.where(lax.broadcasted_iota(jnp.int32, (n, n), 0) == target, 1.0, 0.0).astype(jnp.bfloat16)
        sorted_ref[...] = dot(chosen, raw, NN).astype(jnp.bfloat16)
        gram = dot(sorted_ref[:, :width], sorted_ref[:, :width], NT)
        ridge = ATOM_RIDGE * sorted_ref[:, lane(width, PIVOT_ATOMS)].astype(jnp.float32)
        hit = lax.broadcasted_iota(jnp.int32, (n, n), 0) == lax.broadcasted_iota(jnp.int32, (n, n), 1)
        w_ref[...] = gram * gram + jnp.where(hit, ridge, 0.0)

    at = pl.multiple_of(k * BLOCK, BLOCK)
    rows_ref[...] = sorted_ref[pl.ds(at, BLOCK), :]
    mat_ref[...] = w_ref[pl.ds(at, BLOCK), pl.ds(at, BLOCK)]
    eliminate(mat_ref, inv_ref, out_ref)

    for step in range(count):

        @pl.when(k == step)
        def _(step=step):
            here, after = slice(step * BLOCK, (step + 1) * BLOCK), slice((step + 1) * BLOCK, n)
            inv = split(out_ref[...])
            high_ref[:, here], low_ref[:, here] = inv
            if step:
                left = split(dot3(inv, split(w_ref[here, : step * BLOCK]), NN))
                high_ref[:, : step * BLOCK], low_ref[:, : step * BLOCK] = left
            if step + 1 < count:
                zeros = jnp.zeros((BLOCK, n - (step + 1) * BLOCK), jnp.bfloat16)
                high_ref[:, after], low_ref[:, after] = zeros, zeros
                right = split(dot3(inv, split(w_ref[here, after]), NN))
                lower = split(dot3(split(w_ref[after, here]), inv, NT))
                w_ref[after, after] = w_ref[after, after] - dot3(lower, right, NN)
                w_ref[after, here] = -dot3(lower, inv, NN)
                if step:
                    w_ref[after, : step * BLOCK] = w_ref[after, : step * BLOCK] - dot3(lower, left, NN)


def lane(width, index):
    return slice(width + index, width + index + 1)


def pivot_factor(raw, width):
    n, packed = raw.shape[0], width + EXTRA
    return pl.pallas_call(
        functools.partial(pivot_kernel, n, width),
        grid=(n // BLOCK,),
        out_shape=tuple(pltpu.HBM((n, size), jnp.bfloat16) for size in (packed, n, n)),
        in_specs=[pl.BlockSpec(raw.shape, lambda k: (0, 0), pipeline_mode=pl.Buffered(1))],
        out_specs=tuple(pl.BlockSpec((BLOCK, size), lambda k: (k, 0)) for size in (packed, n, n)),
        scratch_shapes=[pltpu.VMEM((n, packed), jnp.bfloat16), pltpu.VMEM((n, n), jnp.float32)]
        + [pltpu.VMEM((BLOCK, BLOCK), jnp.float32)] * 3,
        compiler_params=pltpu.CompilerParams(vmem_limit_bytes=40 << 20),
        name="pivot_factor",
    )(pltpu.with_memory_space_constraint(raw, pltpu.HBM))


def pivot_stored(index, grid_rows, row_group):
    panel = index // NB
    return panel % grid_rows * row_group + panel // grid_rows * NB + index % NB


def final_kernel(
    grid_rows, grid_cols, row_group, width, row_tiles,
    at_ref, rows_ref, pivots_ref, high_ref, low_ref, col_ref, panel_ref, out_ref, wh_ref, wl_ref, ch_ref, cl_ref,
):
    step = pl.program_id(0)
    n = pivots_ref.shape[0]

    @pl.when(step < row_tiles)
    def _():
        tile = panel_ref.shape[0]
        at = pl.ds(pl.multiple_of(step * tile, tile), tile)
        gram = dot(rows_ref[at, :width], pivots_ref[:, :width], NT)
        ridge = ATOM_RIDGE * rows_ref[at, lane(width, OWN_ATOMS)].astype(jnp.float32)
        local = lax.broadcasted_iota(jnp.int32, (tile, n), 0) + step * tile
        pivot = lax.broadcasted_iota(jnp.int32, (tile, n), 1)
        stored = local + at_ref[0] * row_group
        cov = split(gram * gram + jnp.where(stored == pivot_stored(pivot, grid_rows, row_group), ridge, 0.0))
        row_tile = local // NB * grid_rows + at_ref[0]
        parts = []
        for p in range(n // NB):
            here, upto = slice(p * NB, (p + 1) * NB), slice(0, (p + 1) * NB)
            part = dot3([x[:, upto] for x in cov], (high_ref[here, upto], low_ref[here, upto]), NT)
            part = jnp.where(row_tile[:, here] >= p, part, 0.0)
            panel_ref[:, here] = part
            parts.append(split(part))
        panel = [jnp.concatenate([x[i] for x in parts], axis=1) for i in range(2)]
        for p in range(n // NB):
            here, since = slice(p * NB, (p + 1) * NB), slice(p * NB, n)
            part = dot3([x[:, since] for x in panel], (high_ref[since, here], low_ref[since, here]), NN)
            wh_ref[at, here], wl_ref[at, here] = split(part)

    @pl.when(step >= row_tiles)
    def _():
        total, tile = out_ref.shape
        col = lax.broadcasted_iota(jnp.int32, (n, tile), 1) + (step - row_tiles) * tile
        col_stored = (col // row_group * grid_cols + at_ref[1]) * row_group + col % row_group
        row = lax.broadcasted_iota(jnp.int32, (n, tile), 0)
        gram = dot(pivots_ref[:, :width], col_ref[...], NT)
        ridge = ATOM_RIDGE * pivots_ref[:, lane(width, PIVOT_ATOMS)].astype(jnp.float32)
        hit = pivot_stored(row, grid_rows, row_group) == col_stored
        ch_ref[...], cl_ref[...] = split(gram * gram + jnp.where(hit, ridge, 0.0))
        gram = dot(rows_ref[:, :width], col_ref[...], NT)
        ridge = ATOM_RIDGE * rows_ref[:, lane(width, OWN_ATOMS)].astype(jnp.float32)
        hit = row[:total] + at_ref[0] * row_group == col_stored[:total]
        update = dot3((wh_ref[...], wl_ref[...]), (ch_ref[...], cl_ref[...]), NN)
        out_ref[...] = gram * gram + jnp.where(hit, ridge, 0.0) - update


def final(at, rows, pivots, high, low, cols, grid_rows, grid_cols, row_group, width, row_tile=512, col_tile=256):
    count, total, n = rows.shape[0], cols.shape[0], pivots.shape[0]
    row_tiles = count // row_tile
    whole = lambda x: pl.BlockSpec(x.shape, lambda i, at: (0, 0), pipeline_mode=pl.Buffered(1))
    return pl.pallas_call(
        functools.partial(final_kernel, grid_rows, grid_cols, row_group, width, row_tiles),
        grid_spec=pltpu.PrefetchScalarGridSpec(
            num_scalar_prefetch=1,
            grid=(row_tiles + total // col_tile,),
            in_specs=[whole(rows), whole(pivots), whole(high), whole(low)]
            + [pl.BlockSpec((col_tile, width), lambda i, at: (jnp.maximum(i - row_tiles, 0), 0))],
            out_specs=(
                pl.BlockSpec((row_tile, n), lambda i, at: (jnp.minimum(i, row_tiles - 1), 0)),
                pl.BlockSpec((count, col_tile), lambda i, at: (0, jnp.maximum(i - row_tiles, 0))),
            ),
            scratch_shapes=[pltpu.VMEM((count, n), jnp.bfloat16)] * 2 + [pltpu.VMEM((n, col_tile), jnp.bfloat16)] * 2,
        ),
        out_shape=(
            jax.ShapeDtypeStruct((count, n), jnp.float32),
            jax.ShapeDtypeStruct((count, total), jnp.float32),
        ),
        compiler_params=pltpu.CompilerParams(vmem_limit_bytes=52 << 20),
        name="final",
    )(at, pltpu.with_memory_space_constraint(rows, pltpu.HBM), pivots, high, low, cols)


def in_block_order(rows, place):
    pick = lax.broadcasted_iota(jnp.int32, (rows.shape[0], rows.shape[0]), 0) == place.astype(jnp.int32)[None, :]
    return dot(pick.astype(jnp.bfloat16), rows, NN).astype(jnp.bfloat16)


def body(spectra, projection, kernel_slot, env_image, image_atoms):
    grid_rows = lax.axis_size("row")
    grid_cols = lax.axis_size("col")
    devices = grid_rows * grid_cols
    per_device = spectra.shape[0]
    width = projection.shape[1]
    row_group = per_device * grid_cols
    both = ("row", "col")
    projected = jnp.dot(spectra, projection, preferred_element_type=jnp.float32)
    factor = lax.rsqrt(
        jnp.mean(projected * projected, axis=1, keepdims=True) + NORM_EPS
    ) * width ** (-0.5)
    unit_rows = (projected * factor).astype(jnp.bfloat16)

    images = jnp.arange(image_atoms.shape[0], dtype=jnp.int32)
    atoms = jnp.sum(jnp.where(env_image[:, None] == images[None, :], image_atoms[None, :], 0), axis=1)
    extra_lane = jnp.arange(EXTRA, dtype=jnp.int32)[None, :]
    extra = jnp.where(extra_lane == 0, (kernel_slot % per_device)[:, None], atoms[:, None])
    packed = jnp.concatenate([unit_rows, extra.astype(jnp.bfloat16)], axis=1)

    block = kernel_slot // per_device
    blocks = jnp.arange(devices, dtype=jnp.int32)
    tile_blocks = NB // per_device
    group_blocks = row_group // per_device
    pivot_block = []
    for panel_index in range(PANELS):
        first = panel_index % grid_rows * group_blocks + panel_index // grid_rows * tile_blocks
        pivot_block += [first + i for i in range(tile_blocks)]
    pivot_block = jnp.stack([jnp.int32(i) for i in pivot_block])
    pivot_rows = dot((pivot_block[:, None] == block[None, :]).astype(jnp.bfloat16), packed, NN).astype(jnp.bfloat16)
    count = pivot_rows.shape[0]
    dest_row, dest_col = blocks // grid_cols, blocks % grid_cols
    turned_block = (dest_col + grid_cols * (dest_row // grid_cols)) * grid_cols + dest_row % grid_cols
    turned = dot((turned_block[:, None] == block[None, :]).astype(jnp.bfloat16), packed, NN).astype(jnp.bfloat16)
    own = dot((blocks[:, None] == block[None, :]).astype(jnp.bfloat16), packed, NN).astype(jnp.bfloat16)
    pair = jnp.concatenate([turned[:, :width], own[:, :width]], axis=1).reshape(devices, count, -1)
    spare = jnp.arange(EXTRA)
    spare = jnp.where(spare == 2, turned[:, width, None], jnp.where(spare == 3, own[:, width, None], own[:, width + 1, None]))
    head = jnp.broadcast_to(pivot_rows[None, :, :width], (devices, count, width))
    middle = jnp.where(jnp.arange(EXTRA) < 2, pivot_rows[None, :, width:], spare[:, None, :])
    parcel = jnp.concatenate([head, middle, pair], axis=2)

    parcel = lax.all_to_all(parcel, both, split_axis=0, concat_axis=0, tiled=True)
    pair = parcel[:, :, width + EXTRA :].reshape(per_device, 2 * width)
    places = parcel[:, 0, width : width + EXTRA]
    turned = in_block_order(pair[:, :width], places[:, 2])
    own = in_block_order(jnp.concatenate([pair[:, width:], places], axis=1), places[:, 3])
    col_rows = lax.all_gather(turned, "row", axis=0, tiled=True)
    row_rows = jnp.broadcast_to(own[None], (grid_cols,) + own.shape)
    row_rows = lax.all_to_all(row_rows, "col", split_axis=0, concat_axis=0)
    row_rows = row_rows.reshape(row_group, -1)
    pivots, high, low = pivot_factor(parcel.reshape(-1, parcel.shape[-1]), width)

    at = jnp.stack([lax.axis_index("row"), lax.axis_index("col")]).astype(jnp.int32)
    return final(at, row_rows, pivots, high, low, col_rows, grid_rows, grid_cols, row_group, width)


def solution(mesh):
    in_specs = (P(("row", "col"), None), P(), P(("row", "col")), P(("row", "col")), P())
    out_specs = (P("row", None), P("row", "col"))
    return jax.shard_map(body, mesh=mesh, in_specs=in_specs, out_specs=out_specs, check_vma=False)
```

time: 302 us -> 186 us (0.62); the launches traced: 297 us -> 185 us
  matrix products: 86.2 us -> 6.67 us
  waiting for transfers between devices: 46.3 us -> 0.04 us
  blocking collectives: 22.8 us -> 49.7 us
  local copies, waits for them, and re-layouts: 12 us -> 5.78 us
  other arithmetic: 6.65 us -> 1.87 us
  starting transfers between devices: 9.49 us -> 5.04 us
  Pallas kernels: 98.5 us -> 102 us
    dot_general x25 -> x5, matrix products: 81.5 us -> 1.91 us  [dot(): lax.dot_general(a, b, (dims, ((), ())), preferred_element_type=jnp.float32)]
    all_to_all x2 -> x1, waiting for transfers between devices: 46.3 us -> 0.01 us  [body(): row_rows = lax.all_to_all(row_rows, 'col', split_axis=0, concat_axis=0)]
    all_to_all x1, blocking collectives: 22.8 us -> 49.7 us  [body(): lax.all_to_all(parcel, both, split_axis=0, concat_axis=0, tiled=True)]
    all_to_all x2 -> x1, starting transfers between devices: 9.24 us -> 5 us  [body(): row_rows = lax.all_to_all(row_rows, 'col', split_axis=0, concat_axis=0)]
    slice x3 -> x9, local copies, waits for them, and re-layouts: 4.65 us -> 0.44 us  [the longest x1 0.18 us: body(): own[:, width, None]]
    pallas_call x1 -> x2, Pallas kernels: 98.5 us -> 102 us  [the longest x1 51.3 us: pivot_factor(): pl.pallas_call(functools.partial(pivot_kernel, n, width), grid=(n // BLOC...]
  transfers between devices with their start and end apart: 4 -> 2, of which waited for: 2 -> 0; matrix products, arithmetic and copies ran while one was open for 16% -> 1% of each run, Pallas kernels for 33% -> 28%
where the time goes in v2:
time: 186 us; the launch traced here: 185 us
  Pallas kernels  102 us (55%)
  blocking collectives  49.7 us (27%)
  between operations  14.2 us (8%)
  matrix products  6.67 us (4%)
  local copies, waits for them, and re-layouts  5.78 us (3%)
  starting transfers between devices  5.04 us (3%)
  other arithmetic  1.87 us (1%)
    pallas_call x1, Pallas kernels, pivot_factor(): pl.pallas_call(functools.partial(pivot_kernel, n, width), grid=(n // BLOC...  51.3 us
    pallas_call x1, Pallas kernels, final(): pl.pallas_call(functools.partial(final_kernel, grid_rows, grid_cols, row_...  50.8 us
    all_to_all x1, blocking collectives, body(): lax.all_to_all(parcel, both, split_axis=0, concat_axis=0, tiled=True)  49.7 us
    all_to_all x1, starting transfers between devices, body(): row_rows = lax.all_to_all(row_rows, 'col', split_axis=0, concat_axis=0)  5 us
    dot_general x1, matrix products, body(): projected = jnp.dot(spectra, projection, preferred_element_type=jnp.float32)  4.76 us
  transfers between devices with their start and end apart: 2, of which 0 were waited for; matrix products, arithmetic and copies ran while one was open for 1% of the time, Pallas kernels for 28%

profile of v2, /device:TPU:1, one launch (start us, length us, event | category | flops | bytes accessed | tf_op | source)
XLA Modules:
  0.0 185.5 jit_solution(10176458714600611146)
XLA Ops:
  7.3 0.7 and_select_fusion.5
  8.0 0.4 copy-done
  8.4 4.8 %multiply_reduce_fusion = (f32[128]{0:T(128)S(1)}, f32[128,1024]{1,0:T(8,128)S(1)}) fusion(bf16[128,4096]{1,0:T(8,128)(2,1)S(1)} %copy-done, bf16[4096,1024]{1,0:T(8,128)(2,1)} %param.6), kind=kOutput, calls=%fused_computation.10 | convolution fusion | flops 1074003840 | bytes 9961984 | tf_op jit(solution)/shard_map/dot_general | solution.py:246
  13.2 0.2 select_reduce_fusion
  13.6 0.2 convolution_convert_fusion.3
  13.8 0.2 convolution_convert_fusion.1
  14.1 0.3 convolution_convert_fusion.2
  14.4 0.1 slice_reduce_fusion.2
  14.5 0.2 slice_reduce_fusion.1
  14.8 0.1 copy.14
  14.9 0.1 select_select_fusion
  15.1 0.2 broadcast_in_dim.127
  15.3 0.3 pad_maximum_fusion
  15.6 49.7 %all_to_all.10 = bf16[128,8,1408]{2,1,0:T(8,128)(2,1)S(1)} all-to-all(bf16[128,8,1408]{2,1,0:T(8,128)(2,1)S(1)} %pad_maximum_fusion), channel_id=1, replica_groups=mesh['row'=16,'col'=8] {'row','col'}, dimensions={0} | all-to-all | bytes 5767168 | tf_op jit(solution)/shard_map/all_to_all | solution.py:280
  65.4 0.2 convert_reduce_fusion
  65.6 1.3 copy-done.1
  66.9 0.1 copy.15
  67.0 0.9 convolution_convert_fusion.4
  68.0 0.2 convolution_convert_fusion
  68.3 1.7 broadcast_in_dim.139
  70.0 5.0 %all-to-all-start.1 = ((bf16[8,128,1152]{2,1,0:T(8,128)(2,1)}), bf16[8,128,1152]{2,1,0:T(8,128)(2,1)S(1)}, u32[]{:S(2)}, u32[]{:S(2)}) async-start(bf16[8,128,1152]{2,1,0:T(8,128)(2,1)} %broadcast_in_dim.139), calls=%async_computation.1 | async-start | bytes 4718592 | tf_op jit(solution)/shard_map/all_to_all | solution.py:287
  75.1 51.3 %pivot_factor.1 = (bf16[1024,1152]{1,0:T(8,128)(2,1)}, bf16[1024,1024]{1,0:T(8,128)(2,1)}, bf16[1024,1024]{1,0:T(8,128)(2,1)}) custom-call(bf16[1024,1408]{1,0:T(8,128)(2,1)} %bitcast.13), custom_call_target="tpu_custom_call" | custom-call | tf_op jit(solution)/shard_map/pivot_factor/pallas_call | solution.py:141
  126.4 1.4 copy-done.2
  127.8 50.8 %final.1 = (f32[1024,1024]{1,0:T(8,128)}, f32[1024,2048]{1,0:T(8,128)}) custom-call(s32[2]{0:T(128)S(1)} %pad_add_fusion.at_ref, bf16[1024,1152]{1,0:T(8,128)(2,1)} %bitcast.14, bf16[1024,1152]{1,0:T(8,128)(2,1)} %get-tuple-element.5.pivots_ref, bf16[1024,1024]{1,0:T(8,128)(2,1)} %get-tuple-element.6.high_ref, bf16[1024,1024]{1,0:T(8,128)(2,1)} %get-tuple-element.7.low_ref, ...), custom_call_target="tpu_custom_call" | custom-call | tf_op jit(solution)/shard_map/final/pallas_call | solution.py:211
  (30 shorter events, 0.6 us)
Async XLA Ops:
  7.2 1.2 copy-start
  7.2 119.2 %all-gather.2.cloned.1.call-start = ((), (), s32[]{:S(2)}) async-start(), calls=%async_computation.2 | async-start | bytes 4456448 | tf_op jit(solution)/shard_map/all_gather | solution.py:285
  8.4 4.8 %copy-start.3 = (s32[1024]{0:T(1024)S(1)}, s32[1024]{0:T(1024)}, u32[]{:S(2)}) copy-start(s32[1024]{0:T(1024)} %param.9) | copy-start | bytes 12292
  8.4 4.8 %copy-start.4 = (s32[128]{0:T(128)S(1)}, s32[128]{0:T(128)}, u32[]{:S(2)}) copy-start(s32[128]{0:T(128)} %param.8) | copy-start | bytes 1540
  8.4 5.2 %copy-start.5 = (s32[8]{0:T(128)S(1)}, s32[8]{0:T(128)}, u32[]{:S(2)}) copy-start(s32[8]{0:T(128)} %constant.75.clone.1) | copy-start | bytes 100
  65.3 1.6 copy-start.1
  70.0 56.4 %all-to-all-start.1 = ((bf16[8,128,1152]{2,1,0:T(8,128)(2,1)}), bf16[8,128,1152]{2,1,0:T(8,128)(2,1)S(1)}, u32[]{:S(2)}, u32[]{:S(2)}) async-start(bf16[8,128,1152]{2,1,0:T(8,128)(2,1)} %broadcast_in_dim.139), calls=%async_computation.1 | async-start | bytes 4718592 | tf_op jit(solution)/shard_map/all_to_all | solution.py:287
  126.4 1.4 copy-start.2
Sparse Core Ops, SparseCore 0:
  68.1 47.3 all-gather.1

commit v3 on v2

--- a/solution.py
+++ b/solution.py
@@ -15,6 +15,7 @@
 PIVOT_ATOMS = 1
 OWN_ATOMS = 4
 BLOCK = 128
+PIECE = 256
 NN = ((1,), (0,))
 NT = ((1,), (1,))
 
@@ -58,13 +59,11 @@
             a, b, c = wide(c0[s : s + 1]), wide(c0[s + 1 : s + 2]), wide(c1[s + 1 : s + 2])
             det = a * c - b * b
             r = 1.0 / det
-            ar, br, cr = a * r, b * r, c * r
-            u, w = c0 * cr - c1 * br, c1 * ar - c0 * br
-            u = jnp.where(sub == s, 1.0 - cr, jnp.where(sub == s + 1, br, u))
-            w = jnp.where(sub == s, br, jnp.where(sub == s + 1, 1.0 - ar, w))
+            c0, c1 = c0 - jnp.where(sub == s, 1.0, 0.0), c1 - jnp.where(sub == s + 1, 1.0, 0.0)
+            u, w = c0 * c - c1 * b, c1 * a - c0 * b
 
             def apply(x):
-                return x - (u * wide(x[s : s + 1]) + w * wide(x[s + 1 : s + 2]))
+                return x - (u * wide(x[s : s + 1]) + w * wide(x[s + 1 : s + 2])) * r
 
             for k in range(s + 2, 8):
                 cols[k] = apply(cols[k])
@@ -119,17 +118,30 @@
             inv = split(out_ref[...])
             high_ref[:, here], low_ref[:, here] = inv
             if step:
-                left = split(dot3(inv, split(w_ref[here, : step * BLOCK]), NN))
+                left = split(dot(by_lhs(inv), by_rhs(split(w_ref[here, : step * BLOCK]), 0), NN))
                 high_ref[:, : step * BLOCK], low_ref[:, : step * BLOCK] = left
             if step + 1 < count:
                 zeros = jnp.zeros((BLOCK, n - (step + 1) * BLOCK), jnp.bfloat16)
                 high_ref[:, after], low_ref[:, after] = zeros, zeros
-                right = split(dot3(inv, split(w_ref[here, after]), NN))
-                lower = split(dot3(split(w_ref[after, here]), inv, NT))
-                w_ref[after, after] = w_ref[after, after] - dot3(lower, right, NN)
-                w_ref[after, here] = -dot3(lower, inv, NN)
+                lower = split(dot(by_lhs(split(w_ref[after, here])), by_rhs(inv, 1), NT))
+                lhs, rhs = by_lhs(lower), by_rhs(lower, 1)
+                for first in range((step + 1) * BLOCK, n, 2 * BLOCK):
+                    last = min(first + 2 * BLOCK, n)
+                    skip = first - (step + 1) * BLOCK
+                    w_ref[first:, first:last] = w_ref[first:, first:last] - dot(lhs[skip:], rhs[skip : skip + last - first], NT)
+                w_ref[after, here] = -dot(lhs, by_rhs(inv, 0), NN)
                 if step:
-                    w_ref[after, : step * BLOCK] = w_ref[after, : step * BLOCK] - dot3(lower, left, NN)
+                    w_ref[after, : step * BLOCK] = w_ref[after, : step * BLOCK] - dot(lhs, by_rhs(left, 0), NN)
+
+
+def by_lhs(parts):
+    high, low = parts
+    return jnp.concatenate([high, high, low], axis=1)
+
+
+def by_rhs(parts, axis):
+    high, low = parts
+    return jnp.concatenate([high, low, high], axis=axis)
 
 
 def lane(width, index):
@@ -158,7 +170,7 @@
 
 def final_kernel(
     grid_rows, grid_cols, row_group, width, row_tiles,
-    at_ref, rows_ref, pivots_ref, high_ref, low_ref, col_ref, panel_ref, out_ref, wh_ref, wl_ref, ch_ref, cl_ref,
+    at_ref, rows_ref, pivots_ref, high_ref, low_ref, col_ref, panel_ref, out_ref, w_ref, c_ref,
 ):
     step = pl.program_id(0)
     n = pivots_ref.shape[0]
@@ -175,17 +187,20 @@
         cov = split(gram * gram + jnp.where(stored == pivot_stored(pivot, grid_rows, row_group), ridge, 0.0))
         row_tile = local // NB * grid_rows + at_ref[0]
         parts = []
-        for p in range(n // NB):
-            here, upto = slice(p * NB, (p + 1) * NB), slice(0, (p + 1) * NB)
-            part = dot3([x[:, upto] for x in cov], (high_ref[here, upto], low_ref[here, upto]), NT)
-            part = jnp.where(row_tile[:, here] >= p, part, 0.0)
+        for p in range(n // PIECE):
+            here, upto = slice(p * PIECE, (p + 1) * PIECE), slice(0, (p + 1) * PIECE)
+            part = dot(by_lhs([x[:, upto] for x in cov]), by_rhs((high_ref[here, upto], low_ref[here, upto]), 1), NT)
+            part = jnp.where(row_tile[:, here] >= p * PIECE // NB, part, 0.0)
             panel_ref[:, here] = part
             parts.append(split(part))
         panel = [jnp.concatenate([x[i] for x in parts], axis=1) for i in range(2)]
-        for p in range(n // NB):
-            here, since = slice(p * NB, (p + 1) * NB), slice(p * NB, n)
-            part = dot3([x[:, since] for x in panel], (high_ref[since, here], low_ref[since, here]), NN)
-            wh_ref[at, here], wl_ref[at, here] = split(part)
+        for p in range(n // PIECE):
+            here, since = slice(p * PIECE, (p + 1) * PIECE), slice(p * PIECE, n)
+            part = dot(by_lhs([x[:, since] for x in panel]), by_rhs((high_ref[since, here], low_ref[since, here]), 0), NN)
+            high, low = split(part)
+            w_ref[at, here] = high
+            w_ref[at, n + p * PIECE : n + (p + 1) * PIECE] = high
+            w_ref[at, 2 * n + p * PIECE : 2 * n + (p + 1) * PIECE] = low
 
     @pl.when(step >= row_tiles)
     def _():
@@ -196,15 +211,15 @@
         gram = dot(pivots_ref[:, :width], col_ref[...], NT)
         ridge = ATOM_RIDGE * pivots_ref[:, lane(width, PIVOT_ATOMS)].astype(jnp.float32)
         hit = pivot_stored(row, grid_rows, row_group) == col_stored
-        ch_ref[...], cl_ref[...] = split(gram * gram + jnp.where(hit, ridge, 0.0))
+        high, low = split(gram * gram + jnp.where(hit, ridge, 0.0))
+        c_ref[:n], c_ref[n : 2 * n], c_ref[2 * n :] = high, low, high
         gram = dot(rows_ref[:, :width], col_ref[...], NT)
         ridge = ATOM_RIDGE * rows_ref[:, lane(width, OWN_ATOMS)].astype(jnp.float32)
         hit = row[:total] + at_ref[0] * row_group == col_stored[:total]
-        update = dot3((wh_ref[...], wl_ref[...]), (ch_ref[...], cl_ref[...]), NN)
-        out_ref[...] = gram * gram + jnp.where(hit, ridge, 0.0) - update
-
-
-def final(at, rows, pivots, high, low, cols, grid_rows, grid_cols, row_group, width, row_tile=512, col_tile=256):
+        out_ref[...] = gram * gram + jnp.where(hit, ridge, 0.0) - dot(w_ref[...], c_ref[...], NN)
+
+
+def final(at, rows, pivots, high, low, cols, grid_rows, grid_cols, row_group, width, row_tile=512, col_tile=512):
     count, total, n = rows.shape[0], cols.shape[0], pivots.shape[0]
     row_tiles = count // row_tile
     whole = lambda x: pl.BlockSpec(x.shape, lambda i, at: (0, 0), pipeline_mode=pl.Buffered(1))
@@ -219,7 +234,7 @@
                 pl.BlockSpec((row_tile, n), lambda i, at: (jnp.minimum(i, row_tiles - 1), 0)),
                 pl.BlockSpec((count, col_tile), lambda i, at: (0, jnp.maximum(i - row_tiles, 0))),
             ),
-            scratch_shapes=[pltpu.VMEM((count, n), jnp.bfloat16)] * 2 + [pltpu.VMEM((n, col_tile), jnp.bfloat16)] * 2,
+            scratch_shapes=[pltpu.VMEM((count, 3 * n), jnp.bfloat16), pltpu.VMEM((3 * n, col_tile), jnp.bfloat16)],
         ),
         out_shape=(
             jax.ShapeDtypeStruct((count, n), jnp.float32),

time: 186 us -> 167 us (0.90)
  Pallas kernels: 102 us -> 83.4 us
    pallas_call x1, Pallas kernels: 50.8 us -> 41.2 us  [final(): pl.pallas_call(functools.partial(final_kernel, grid_rows, grid_cols, row_...]
    pallas_call x1, Pallas kernels: 51.3 us -> 42.2 us  [pivot_factor(): pl.pallas_call(functools.partial(pivot_kernel, n, width), grid=(n // BLOC...]
  transfers between devices with their start and end apart: 2 -> 2, of which waited for: 0 -> 0; matrix products, arithmetic and copies ran while one was open for 1% -> 1% of each run, Pallas kernels for 28% -> 25%
where the time goes in v3:
time: 167 us
  Pallas kernels  83.4 us (50%)
  blocking collectives  49.7 us (30%)
  between operations  14.2 us (9%)
  matrix products  6.67 us (4%)
  local copies, waits for them, and re-layouts  5.78 us (3%)
  starting transfers between devices  5.04 us (3%)
  other arithmetic  1.87 us (1%)
    all_to_all x1, blocking collectives, body(): lax.all_to_all(parcel, both, split_axis=0, concat_axis=0, tiled=True)  49.7 us
    pallas_call x1, Pallas kernels, pivot_factor(): pl.pallas_call(functools.partial(pivot_kernel, n, width), grid=(n // BLOC...  42.2 us
    pallas_call x1, Pallas kernels, final(): pl.pallas_call(functools.partial(final_kernel, grid_rows, grid_cols, row_...  41.2 us
    all_to_all x1, starting transfers between devices, body(): row_rows = lax.all_to_all(row_rows, 'col', split_axis=0, concat_axis=0)  5 us
    dot_general x1, matrix products, body(): projected = jnp.dot(spectra, projection, preferred_element_type=jnp.float32)  4.76 us
    unnamed x15, local copies, waits for them, and re-layouts  3.38 us
  transfers between devices with their start and end apart: 2, of which 0 were waited for; matrix products, arithmetic and copies ran while one was open for 1% of the time, Pallas kernels for 25%

profile of v3, /device:TPU:1, one launch (start us, length us, event | category | flops | bytes accessed | tf_op | source)
XLA Modules:
  0.0 166.7 jit_solution(15252059907571051686)
XLA Ops:
  7.3 0.7 and_select_fusion.5
  8.0 0.4 copy-done
  8.4 4.8 %multiply_reduce_fusion = (f32[128]{0:T(128)S(1)}, f32[128,1024]{1,0:T(8,128)S(1)}) fusion(bf16[128,4096]{1,0:T(8,128)(2,1)S(1)} %copy-done, bf16[4096,1024]{1,0:T(8,128)(2,1)} %param.6), kind=kOutput, calls=%fused_computation.10 | convolution fusion | flops 1074003840 | bytes 9961984 | tf_op jit(solution)/shard_map/dot_general | solution.py:261
  13.2 0.2 select_reduce_fusion
  13.6 0.2 convolution_convert_fusion.3
  13.8 0.2 convolution_convert_fusion.1
  14.1 0.3 convolution_convert_fusion.2
  14.4 0.1 slice_reduce_fusion.2
  14.5 0.2 slice_reduce_fusion.1
  14.8 0.1 copy.14
  14.9 0.1 select_select_fusion
  15.1 0.2 broadcast_in_dim.127
  15.3 0.3 pad_maximum_fusion
  15.6 49.7 %all_to_all.10 = bf16[128,8,1408]{2,1,0:T(8,128)(2,1)S(1)} all-to-all(bf16[128,8,1408]{2,1,0:T(8,128)(2,1)S(1)} %pad_maximum_fusion), channel_id=1, replica_groups=mesh['row'=16,'col'=8] {'row','col'}, dimensions={0} | all-to-all | bytes 5767168 | tf_op jit(solution)/shard_map/all_to_all | solution.py:295
  65.4 0.2 convert_reduce_fusion
  65.6 1.3 copy-done.1
  66.9 0.1 copy.15
  67.0 0.9 convolution_convert_fusion.4
  68.0 0.2 convolution_convert_fusion
  68.3 1.7 %broadcast_in_dim.139 = bf16[8,128,1152]{2,1,0:T(8,128)(2,1)} broadcast(bf16[128,1152]{1,0:T(8,128)(2,1)S(1)} %convolution_convert_fusion), dimensions={1,2} | broadcast | bytes 2654208 | tf_op jit(solution)/shard_map/broadcast_in_dim | solution.py:301
  70.0 5.0 %all-to-all-start.1 = ((bf16[8,128,1152]{2,1,0:T(8,128)(2,1)}), bf16[8,128,1152]{2,1,0:T(8,128)(2,1)S(1)}, u32[]{:S(2)}, u32[]{:S(2)}) async-start(bf16[8,128,1152]{2,1,0:T(8,128)(2,1)} %broadcast_in_dim.139), calls=%async_computation.1 | async-start | bytes 4718592 | tf_op jit(solution)/shard_map/all_to_all | solution.py:302
  75.1 42.2 %pivot_factor.1 = (bf16[1024,1152]{1,0:T(8,128)(2,1)}, bf16[1024,1024]{1,0:T(8,128)(2,1)}, bf16[1024,1024]{1,0:T(8,128)(2,1)}) custom-call(bf16[1024,1408]{1,0:T(8,128)(2,1)} %bitcast.13), custom_call_target="tpu_custom_call" | custom-call | tf_op jit(solution)/shard_map/pivot_factor/pallas_call | solution.py:153
  117.3 1.4 copy-done.2
  118.7 41.2 %final.1 = (f32[1024,1024]{1,0:T(8,128)}, f32[1024,2048]{1,0:T(8,128)}) custom-call(s32[2]{0:T(128)S(1)} %pad_add_fusion.at_ref, bf16[1024,1152]{1,0:T(8,128)(2,1)} %bitcast.14, bf16[1024,1152]{1,0:T(8,128)(2,1)} %get-tuple-element.5.pivots_ref, bf16[1024,1024]{1,0:T(8,128)(2,1)} %get-tuple-element.6.high_ref, bf16[1024,1024]{1,0:T(8,128)(2,1)} %get-tuple-element.7.low_ref, ...), custom_call_target="tpu_custom_call" | custom-call | tf_op jit(solution)/shard_map/final/pallas_call | solution.py:226
  (30 shorter events, 0.6 us)
Async XLA Ops:
  7.2 1.2 copy-start
  7.2 110.1 %all-gather.2.cloned.1.call-start = ((), (), s32[]{:S(2)}) async-start(), calls=%async_computation.2 | async-start | bytes 4456448 | tf_op jit(solution)/shard_map/all_gather | solution.py:300
  8.4 4.8 %copy-start.3 = (s32[1024]{0:T(1024)S(1)}, s32[1024]{0:T(1024)}, u32[]{:S(2)}) copy-start(s32[1024]{0:T(1024)} %param.9) | copy-start | bytes 12292
  8.4 4.8 %copy-start.4 = (s32[128]{0:T(128)S(1)}, s32[128]{0:T(128)}, u32[]{:S(2)}) copy-start(s32[128]{0:T(128)} %param.8) | copy-start | bytes 1540
  8.4 5.2 %copy-start.5 = (s32[8]{0:T(128)S(1)}, s32[8]{0:T(128)}, u32[]{:S(2)}) copy-start(s32[8]{0:T(128)} %constant.75.clone.1) | copy-start | bytes 100
  65.3 1.6 copy-start.1
  70.0 47.3 %all-to-all-start.1 = ((bf16[8,128,1152]{2,1,0:T(8,128)(2,1)}), bf16[8,128,1152]{2,1,0:T(8,128)(2,1)S(1)}, u32[]{:S(2)}, u32[]{:S(2)}) async-start(bf16[8,128,1152]{2,1,0:T(8,128)(2,1)} %broadcast_in_dim.139), calls=%async_computation.1 | async-start | bytes 4718592 | tf_op jit(solution)/shard_map/all_to_all | solution.py:302
  117.2 1.4 copy-start.2
Sparse Core Ops, SparseCore 0:
  68.1 47.2 all-gather.1

commit v4 on v3

--- a/solution.py
+++ b/solution.py
@@ -6,6 +6,7 @@
 from jax.experimental import pallas as pl
 from jax.experimental.pallas import tpu as pltpu
 from jax.sharding import PartitionSpec as P
+
 
 NB = 512
 PANELS = 2
@@ -25,19 +26,8 @@
     return high, (a - high.astype(jnp.float32)).astype(jnp.bfloat16)
 
 
-def halves(a):
-    high = lax.reduce_precision(a, 8, 7)
-    return high.astype(jnp.bfloat16), (a - high).astype(jnp.bfloat16)
-
-
 def dot(a, b, dims):
     return lax.dot_general(a, b, (dims, ((), ())), preferred_element_type=jnp.float32)
-
-
-def dot3(a, b, dims):
-    a_high, a_low = a
-    b_high, b_low = b
-    return dot(a_high, b_high, dims) + (dot(a_high, b_low, dims) + dot(a_low, b_high, dims))
 
 
 def eliminate(mat_ref, inv_ref, out_ref):
@@ -88,18 +78,27 @@
     return values[0]
 
 
-def pivot_kernel(n, width, raw_ref, rows_ref, high_ref, low_ref, sorted_ref, w_ref, mat_ref, inv_ref, out_ref):
+def pivot_kernel(n, width, core_ref, own_ref, other_ref, rows_ref, high_ref, low_ref, sorted_ref, w_ref, mat_ref, inv_ref, out_ref):
     k = pl.program_id(0)
     count = n // BLOCK
 
     @pl.when(k == 0)
     def _():
-        raw = raw_ref[:, : width + EXTRA]
+        half, share = width // 2, n // 2
         pick = (lax.broadcasted_iota(jnp.int32, (8, EXTRA), 1) == 0).astype(jnp.bfloat16)
-        place = dot(pick, raw[:, width:], NT)[0:1, :].astype(jnp.int32)
-        target = lax.broadcasted_iota(jnp.int32, (1, n), 1) % count * BLOCK + place
-        chosen = jnp.where(lax.broadcasted_iota(jnp.int32, (n, n), 0) == target, 1.0, 0.0).astype(jnp.bfloat16)
-        sorted_ref[...] = dot(chosen, raw, NN).astype(jnp.bfloat16)
+        for source, raw_ref in ((core_ref[0], own_ref), (1 - core_ref[0], other_ref)):
+            here = pl.ds(pl.multiple_of(source * share, share), share)
+            raw = raw_ref[:, : half + EXTRA]
+            place = dot(pick, raw[:, half:], NT)[0:1, :].astype(jnp.int32)
+            line = lax.broadcasted_iota(jnp.int32, (1, n), 1) % count
+            target = line // 2 * BLOCK + place
+            out = lax.broadcasted_iota(jnp.int32, (share, n), 0)
+            left = jnp.where(out == jnp.where(line % 2 == 0, target, -1), 1.0, 0.0).astype(jnp.bfloat16)
+            left = dot(left, raw, NN).astype(jnp.bfloat16)
+            right = jnp.where(out == jnp.where(line % 2 == 1, target, -1), 1.0, 0.0).astype(jnp.bfloat16)
+            sorted_ref[here, :half] = left[:, :half]
+            sorted_ref[here, half:width] = dot(right, raw[:, :half], NN).astype(jnp.bfloat16)
+            sorted_ref[here, width:] = left[:, half:]
         gram = dot(sorted_ref[:, :width], sorted_ref[:, :width], NT)
         ridge = ATOM_RIDGE * sorted_ref[:, lane(width, PIVOT_ATOMS)].astype(jnp.float32)
         hit = lax.broadcasted_iota(jnp.int32, (n, n), 0) == lax.broadcasted_iota(jnp.int32, (n, n), 1)
@@ -148,19 +147,23 @@
     return slice(width + index, width + index + 1)
 
 
-def pivot_factor(raw, width):
-    n, packed = raw.shape[0], width + EXTRA
+def pivot_factor(core, own, other, width):
+    n, packed = own.shape[0], width + EXTRA
+    raw = pl.BlockSpec(own.shape, lambda k, core: (0, 0), pipeline_mode=pl.Buffered(1))
     return pl.pallas_call(
         functools.partial(pivot_kernel, n, width),
-        grid=(n // BLOCK,),
+        grid_spec=pltpu.PrefetchScalarGridSpec(
+            num_scalar_prefetch=1,
+            grid=(n // BLOCK,),
+            in_specs=[raw, raw],
+            out_specs=tuple(pl.BlockSpec((BLOCK, size), lambda k, core: (k, 0)) for size in (packed, n, n)),
+            scratch_shapes=[pltpu.VMEM((n, packed), jnp.bfloat16), pltpu.VMEM((n, n), jnp.float32)]
+            + [pltpu.VMEM((BLOCK, BLOCK), jnp.float32)] * 3,
+        ),
         out_shape=tuple(pltpu.HBM((n, size), jnp.bfloat16) for size in (packed, n, n)),
-        in_specs=[pl.BlockSpec(raw.shape, lambda k: (0, 0), pipeline_mode=pl.Buffered(1))],
-        out_specs=tuple(pl.BlockSpec((BLOCK, size), lambda k: (k, 0)) for size in (packed, n, n)),
-        scratch_shapes=[pltpu.VMEM((n, packed), jnp.bfloat16), pltpu.VMEM((n, n), jnp.float32)]
-        + [pltpu.VMEM((BLOCK, BLOCK), jnp.float32)] * 3,
         compiler_params=pltpu.CompilerParams(vmem_limit_bytes=40 << 20),
         name="pivot_factor",
-    )(pltpu.with_memory_space_constraint(raw, pltpu.HBM))
+    )(core, pltpu.with_memory_space_constraint(own, pltpu.HBM), pltpu.with_memory_space_constraint(other, pltpu.HBM))
 
 
 def pivot_stored(index, grid_rows, row_group):
@@ -285,23 +288,31 @@
     turned_block = (dest_col + grid_cols * (dest_row // grid_cols)) * grid_cols + dest_row % grid_cols
     turned = dot((turned_block[:, None] == block[None, :]).astype(jnp.bfloat16), packed, NN).astype(jnp.bfloat16)
     own = dot((blocks[:, None] == block[None, :]).astype(jnp.bfloat16), packed, NN).astype(jnp.bfloat16)
+    half = width // 2
+    heads = pivot_rows[:, :width].reshape(2, count, half)
+    extras = jnp.repeat(pivot_rows[:, width:], 2, axis=0).reshape(2, count, EXTRA)
+    core = (dest_col % 2)[:, None, None]
     pair = jnp.concatenate([turned[:, :width], own[:, :width]], axis=1).reshape(devices, count, -1)
     spare = jnp.arange(EXTRA)
     spare = jnp.where(spare == 2, turned[:, width, None], jnp.where(spare == 3, own[:, width, None], own[:, width + 1, None]))
-    head = jnp.broadcast_to(pivot_rows[None, :, :width], (devices, count, width))
-    middle = jnp.where(jnp.arange(EXTRA) < 2, pivot_rows[None, :, width:], spare[:, None, :])
+    head = jnp.where(core == 0, heads[None, 0], heads[None, 1])
+    middle = jnp.where(core == 0, extras[None, 0], extras[None, 1])
+    middle = jnp.where(jnp.arange(EXTRA) < 2, middle, spare[:, None, :])
     parcel = jnp.concatenate([head, middle, pair], axis=2)
 
     parcel = lax.all_to_all(parcel, both, split_axis=0, concat_axis=0, tiled=True)
-    pair = parcel[:, :, width + EXTRA :].reshape(per_device, 2 * width)
-    places = parcel[:, 0, width : width + EXTRA]
+    lines = parcel.reshape(devices * count, -1)
+    partner = lax.ppermute(lines, "col", [(i, i + 1 - i % 2 * 2) for i in range(grid_cols)])
+    pair = parcel[:, :, half + EXTRA :].reshape(per_device, 2 * width)
+    places = parcel[:, 0, half : half + EXTRA]
     turned = in_block_order(pair[:, :width], places[:, 2])
     own = in_block_order(jnp.concatenate([pair[:, width:], places], axis=1), places[:, 3])
     col_rows = lax.all_gather(turned, "row", axis=0, tiled=True)
     row_rows = jnp.broadcast_to(own[None], (grid_cols,) + own.shape)
     row_rows = lax.all_to_all(row_rows, "col", split_axis=0, concat_axis=0)
     row_rows = row_rows.reshape(row_group, -1)
-    pivots, high, low = pivot_factor(parcel.reshape(-1, parcel.shape[-1]), width)
+    core = (lax.axis_index("col") % 2).astype(jnp.int32)[None]
+    pivots, high, low = pivot_factor(core, lines, partner, width)
 
     at = jnp.stack([lax.axis_index("row"), lax.axis_index("col")]).astype(jnp.int32)
     return final(at, row_rows, pivots, high, low, col_rows, grid_rows, grid_cols, row_group, width)

time: 167 us -> 158 us (0.946)
  blocking collectives: 49.7 us -> 38.6 us
  waiting for transfers between devices: 0.04 us -> 3.91 us
  local copies, waits for them, and re-layouts: 5.78 us -> 2.85 us
    all_to_all x1, blocking collectives: 49.7 us -> 38.6 us  [body(): lax.all_to_all(parcel, both, split_axis=0, concat_axis=0, tiled=True)]
    ppermute x0 -> x1, waiting for transfers between devices: none -> 3.88 us  [body(): lax.ppermute(lines, 'col', [(i, i + 1 - i % 2 * 2) for i in range(grid_co...]
    unnamed x15 -> x13, local copies, waits for them, and re-layouts: 3.38 us -> 0.66 us
  transfers between devices with their start and end apart: 2 -> 3, of which waited for: 0 -> 1; matrix products, arithmetic and copies ran while one was open for 1% -> 1% of each run, Pallas kernels for 25% -> 27%
where the time goes in v4:
time: 158 us
  Pallas kernels  83.7 us (53%)
  blocking collectives  38.6 us (24%)
  between operations  14.3 us (9%)
  matrix products  6.65 us (4%)
  starting transfers between devices  5.88 us (4%)
  waiting for transfers between devices  3.91 us (2%)
  local copies, waits for them, and re-layouts  2.85 us (2%)
  other arithmetic  2.15 us (1%)
    pallas_call x1, Pallas kernels, pivot_factor(): pl.pallas_call(functools.partial(pivot_kernel, n, width), grid_spec=pltpu...  42.5 us
    pallas_call x1, Pallas kernels, final(): pl.pallas_call(functools.partial(final_kernel, grid_rows, grid_cols, row_...  41.2 us
    all_to_all x1, blocking collectives, body(): lax.all_to_all(parcel, both, split_axis=0, concat_axis=0, tiled=True)  38.6 us
    all_to_all x1, starting transfers between devices, body(): row_rows = lax.all_to_all(row_rows, 'col', split_axis=0, concat_axis=0)  5.63 us
    dot_general x1, matrix products, body(): projected = jnp.dot(spectra, projection, preferred_element_type=jnp.float32)  4.76 us
    ppermute x1, waiting for transfers between devices, body(): lax.ppermute(lines, 'col', [(i, i + 1 - i % 2 * 2) for i in range(grid_co...  3.88 us
  transfers between devices with their start and end apart: 3, of which 1 were waited for; matrix products, arithmetic and copies ran while one was open for 1% of the time, Pallas kernels for 27%

profile of v4, /device:TPU:1, one launch (start us, length us, event | category | flops | bytes accessed | tf_op | source)
XLA Modules:
  0.0 158.0 jit_solution(11952796260910645681)
XLA Ops:
  7.3 0.7 and_select_fusion.4
  8.0 0.4 copy-done
  8.4 4.8 %multiply_reduce_fusion = (f32[128]{0:T(128)S(1)}, f32[128,1024]{1,0:T(8,128)S(1)}) fusion(bf16[128,4096]{1,0:T(8,128)(2,1)S(1)} %copy-done, bf16[4096,1024]{1,0:T(8,128)(2,1)} %param.6), kind=kOutput, calls=%fused_computation.11 | convolution fusion | flops 1074003840 | bytes 9961984 | tf_op jit(solution)/shard_map/dot_general | solution.py:264
  13.2 0.2 select_reduce_fusion
  13.6 0.2 convolution_convert_fusion.3
  13.9 0.2 convolution_convert_fusion.1
  14.1 0.3 convolution_convert_fusion.2
  14.5 0.2 slice_reduce_fusion.1
  14.8 0.1 copy.14
  15.0 0.2 broadcast_select_fusion
  15.2 0.1 select_select_fusion.1
  15.3 0.2 select_select_fusion
  15.5 0.2 pad_maximum_fusion
  15.7 38.6 %all_to_all.10 = bf16[128,8,896]{2,1,0:T(8,128)(2,1)S(1)} all-to-all(bf16[128,8,896]{2,1,0:T(8,128)(2,1)S(1)} %pad_maximum_fusion), channel_id=1, replica_groups=mesh['row'=16,'col'=8] {'row','col'}, dimensions={0} | all-to-all | bytes 3670016 | tf_op jit(solution)/shard_map/all_to_all | solution.py:303
  54.4 0.2 convert_reduce_fusion
  54.6 0.1 copy.15
  54.7 0.9 convolution_convert_fusion.4
  55.7 0.2 convolution_convert_fusion
  56.0 1.7 %broadcast_in_dim.199 = bf16[8,128,1152]{2,1,0:T(8,128)(2,1)} broadcast(bf16[128,1152]{1,0:T(8,128)(2,1)S(1)} %convolution_convert_fusion), dimensions={1,2} | broadcast | bytes 2654208 | tf_op jit(solution)/shard_map/broadcast_in_dim | solution.py:311
  57.7 5.6 %all-to-all-start.1 = ((bf16[8,128,1152]{2,1,0:T(8,128)(2,1)}), bf16[8,128,1152]{2,1,0:T(8,128)(2,1)}, u32[]{:S(2)}, u32[]{:S(2)}) async-start(bf16[8,128,1152]{2,1,0:T(8,128)(2,1)} %broadcast_in_dim.199), calls=%async_computation.1 | async-start | bytes 4718592 | tf_op jit(solution)/shard_map/all_to_all | solution.py:312
  63.3 0.2 collective-permute-start
  63.6 3.9 %collective-permute-done.other_ref = bf16[1024,896]{1,0:T(8,128)(2,1)} collective-permute-done((bf16[1024,896]{1,0:T(8,128)(2,1)S(1)}, bf16[1024,896]{1,0:T(8,128)(2,1)}, u32[]{:S(2)}, u32[]{:S(2)}) %collective-permute-start) | collective-permute-done | bytes 1835040 | tf_op jit(solution)/shard_map/ppermute | solution.py:305
  67.5 42.5 %pivot_factor.1 = (bf16[1024,1152]{1,0:T(8,128)(2,1)}, bf16[1024,1024]{1,0:T(8,128)(2,1)}, bf16[1024,1024]{1,0:T(8,128)(2,1)}) custom-call(s32[1]{0:T(128)} %bitcast.6.core_ref, bf16[1024,896]{1,0:T(8,128)(2,1)} %bitcast.17, bf16[1024,896]{1,0:T(8,128)(2,1)} %collective-permute-done.other_ref), custom_call_target="tpu_custom_call" | custom-call | tf_op jit(solution)/shard_map/pivot_factor/pallas_call | solution.py:153
  109.9 41.2 %final.1 = (f32[1024,1024]{1,0:T(8,128)}, f32[1024,2048]{1,0:T(8,128)}) custom-call(s32[2]{0:T(128)S(1)} %pad_add_fusion.at_ref, bf16[1024,1152]{1,0:T(8,128)(2,1)} %bitcast.5.rows_ref, bf16[1024,1152]{1,0:T(8,128)(2,1)} %get-tuple-element.5.pivots_ref, bf16[1024,1024]{1,0:T(8,128)(2,1)} %get-tuple-element.6.high_ref, ...), custom_call_target="tpu_custom_call" | custom-call | tf_op jit(solution)/shard_map/final/pallas_call | solution.py:229
  (34 shorter events, 0.8 us)
Async XLA Ops:
  7.2 1.2 copy-start
  7.2 102.8 %all-gather.2.cloned.1.call-start = ((), (), s32[]{:S(2)}) async-start(), calls=%async_computation.2 | async-start | bytes 4456448 | tf_op jit(solution)/shard_map/all_gather | solution.py:310
  8.4 4.8 %copy-start.2 = (s32[1024]{0:T(1024)S(1)}, s32[1024]{0:T(1024)}, u32[]{:S(2)}) copy-start(s32[1024]{0:T(1024)} %param.9) | copy-start | bytes 12292
  8.4 4.8 %copy-start.3 = (s32[128]{0:T(128)S(1)}, s32[128]{0:T(128)}, u32[]{:S(2)}) copy-start(s32[128]{0:T(128)} %param.8) | copy-start | bytes 1540
  8.4 5.2 %copy-start.4 = (s32[8]{0:T(128)S(1)}, s32[8]{0:T(128)}, u32[]{:S(2)}) copy-start(s32[8]{0:T(128)} %constant.99.clone.1) | copy-start | bytes 100
  54.3 9.0 %copy-start.1 = (bf16[128,8,896]{2,1,0:T(8,128)(2,1)}, bf16[128,8,896]{2,1,0:T(8,128)(2,1)S(1)}, u32[]{:S(2)}) copy-start(bf16[128,8,896]{2,1,0:T(8,128)(2,1)S(1)} %all_to_all.10) | copy-start | bytes 5505028
  57.7 52.3 %all-to-all-start.1 = ((bf16[8,128,1152]{2,1,0:T(8,128)(2,1)}), bf16[8,128,1152]{2,1,0:T(8,128)(2,1)}, u32[]{:S(2)}, u32[]{:S(2)}) async-start(bf16[8,128,1152]{2,1,0:T(8,128)(2,1)} %broadcast_in_dim.199), calls=%async_computation.1 | async-start | bytes 4718592 | tf_op jit(solution)/shard_map/all_to_all | solution.py:312
  63.3 4.2 %collective-permute-start = (bf16[1024,896]{1,0:T(8,128)(2,1)S(1)}, bf16[1024,896]{1,0:T(8,128)(2,1)}, u32[]{:S(2)}, u32[]{:S(2)}) collective-permute-start(bf16[1024,896]{1,0:T(8,128)(2,1)S(1)} %bitcast.16), channel_id=1, source_target_pairs={{0,1},{1,0},{2,3},{3,2},{4,5},{5,4},{6,7},{7,6},{8,9},{9,8},{10,11... | collective-permute-start | bytes 5505032 | tf_op jit(solution)/shard_map/ppermute | solution.py:305
Sparse Core Ops, SparseCore 0:
  55.8 47.1 all-gather.1

commit v5 on v4

--- a/solution.py
+++ b/solution.py
@@ -88,7 +88,7 @@
         pick = (lax.broadcasted_iota(jnp.int32, (8, EXTRA), 1) == 0).astype(jnp.bfloat16)
         for source, raw_ref in ((core_ref[0], own_ref), (1 - core_ref[0], other_ref)):
             here = pl.ds(pl.multiple_of(source * share, share), share)
-            raw = raw_ref[:, : half + EXTRA]
+            raw = raw_ref[...]
             place = dot(pick, raw[:, half:], NT)[0:1, :].astype(jnp.int32)
             line = lax.broadcasted_iota(jnp.int32, (1, n), 1) % count
             target = line // 2 * BLOCK + place
@@ -99,10 +99,12 @@
             sorted_ref[here, :half] = left[:, :half]
             sorted_ref[here, half:width] = dot(right, raw[:, :half], NN).astype(jnp.bfloat16)
             sorted_ref[here, width:] = left[:, half:]
-        gram = dot(sorted_ref[:, :width], sorted_ref[:, :width], NT)
-        ridge = ATOM_RIDGE * sorted_ref[:, lane(width, PIVOT_ATOMS)].astype(jnp.float32)
-        hit = lax.broadcasted_iota(jnp.int32, (n, n), 0) == lax.broadcasted_iota(jnp.int32, (n, n), 1)
-        w_ref[...] = gram * gram + jnp.where(hit, ridge, 0.0)
+        for first in range(0, n, PIECE):
+            here = slice(first, first + PIECE)
+            gram = dot(sorted_ref[first:, :width], sorted_ref[here, :width], NT)
+            ridge = ATOM_RIDGE * sorted_ref[first:, lane(width, PIVOT_ATOMS)].astype(jnp.float32)
+            hit = lax.broadcasted_iota(jnp.int32, gram.shape, 0) == lax.broadcasted_iota(jnp.int32, gram.shape, 1)
+            w_ref[first:, here] = gram * gram + jnp.where(hit, ridge, 0.0)
 
     at = pl.multiple_of(k * BLOCK, BLOCK)
     rows_ref[...] = sorted_ref[pl.ds(at, BLOCK), :]
@@ -149,7 +151,7 @@
 
 def pivot_factor(core, own, other, width):
     n, packed = own.shape[0], width + EXTRA
-    raw = pl.BlockSpec(own.shape, lambda k, core: (0, 0), pipeline_mode=pl.Buffered(1))
+    raw = pl.BlockSpec((n, width // 2 + EXTRA), lambda k, core: (0, 0), pipeline_mode=pl.Buffered(1))
     return pl.pallas_call(
         functools.partial(pivot_kernel, n, width),
         grid_spec=pltpu.PrefetchScalarGridSpec(

time: 158 us -> 157 us (level)
  transfers between devices with their start and end apart: 3 -> 3, of which waited for: 1 -> 1; matrix products, arithmetic and copies ran while one was open for 1% -> 1% of each run, Pallas kernels for 27% -> 26%
where the time goes in v5:
time: 157 us
  Pallas kernels  82.5 us (53%)
  blocking collectives  38.6 us (25%)
  between operations  14.3 us (9%)
  matrix products  6.65 us (4%)
  starting transfers between devices  5.88 us (4%)
  waiting for transfers between devices  3.91 us (2%)
  local copies, waits for them, and re-layouts  2.85 us (2%)
  other arithmetic  2.15 us (1%)
    pallas_call x1, Pallas kernels, pivot_factor(): pl.pallas_call(functools.partial(pivot_kernel, n, width), grid_spec=pltpu...  41.3 us
    pallas_call x1, Pallas kernels, final(): pl.pallas_call(functools.partial(final_kernel, grid_rows, grid_cols, row_...  41.2 us
    all_to_all x1, blocking collectives, body(): lax.all_to_all(parcel, both, split_axis=0, concat_axis=0, tiled=True)  38.6 us
    all_to_all x1, starting transfers between devices, body(): row_rows = lax.all_to_all(row_rows, 'col', split_axis=0, concat_axis=0)  5.63 us
    dot_general x1, matrix products, body(): projected = jnp.dot(spectra, projection, preferred_element_type=jnp.float32)  4.76 us
    ppermute x1, waiting for transfers between devices, body(): lax.ppermute(lines, 'col', [(i, i + 1 - i % 2 * 2) for i in range(grid_co...  3.88 us
  transfers between devices with their start and end apart: 3, of which 1 were waited for; matrix products, arithmetic and copies ran while one was open for 1% of the time, Pallas kernels for 26%

profile of v5, /device:TPU:1, one launch (start us, length us, event | category | flops | bytes accessed | tf_op | source)
XLA Modules:
  0.0 156.8 jit_solution(10681901242551940097)
XLA Ops:
  7.3 0.7 and_select_fusion.4
  8.0 0.4 copy-done
  8.4 4.8 %multiply_reduce_fusion = (f32[128]{0:T(128)S(1)}, f32[128,1024]{1,0:T(8,128)S(1)}) fusion(bf16[128,4096]{1,0:T(8,128)(2,1)S(1)} %copy-done, bf16[4096,1024]{1,0:T(8,128)(2,1)} %param.6), kind=kOutput, calls=%fused_computation.11 | convolution fusion | flops 1074003840 | bytes 9961984 | tf_op jit(solution)/shard_map/dot_general | solution.py:266
  13.2 0.2 select_reduce_fusion
  13.6 0.2 convolution_convert_fusion.3
  13.9 0.2 convolution_convert_fusion.1
  14.1 0.3 convolution_convert_fusion.2
  14.5 0.2 slice_reduce_fusion.1
  14.8 0.1 copy.14
  15.0 0.2 broadcast_select_fusion
  15.2 0.1 select_select_fusion.1
  15.3 0.2 select_select_fusion
  15.5 0.2 pad_maximum_fusion
  15.7 38.6 %all_to_all.10 = bf16[128,8,896]{2,1,0:T(8,128)(2,1)S(1)} all-to-all(bf16[128,8,896]{2,1,0:T(8,128)(2,1)S(1)} %pad_maximum_fusion), channel_id=1, replica_groups=mesh['row'=16,'col'=8] {'row','col'}, dimensions={0} | all-to-all | bytes 3670016 | tf_op jit(solution)/shard_map/all_to_all | solution.py:305
  54.4 0.2 convert_reduce_fusion
  54.6 0.1 copy.15
  54.7 0.9 convolution_convert_fusion.4
  55.7 0.2 convolution_convert_fusion
  56.0 1.7 %broadcast_in_dim.199 = bf16[8,128,1152]{2,1,0:T(8,128)(2,1)} broadcast(bf16[128,1152]{1,0:T(8,128)(2,1)S(1)} %convolution_convert_fusion), dimensions={1,2} | broadcast | bytes 2654208 | tf_op jit(solution)/shard_map/broadcast_in_dim | solution.py:313
  57.7 5.6 %all-to-all-start.1 = ((bf16[8,128,1152]{2,1,0:T(8,128)(2,1)}), bf16[8,128,1152]{2,1,0:T(8,128)(2,1)}, u32[]{:S(2)}, u32[]{:S(2)}) async-start(bf16[8,128,1152]{2,1,0:T(8,128)(2,1)} %broadcast_in_dim.199), calls=%async_computation.1 | async-start | bytes 4718592 | tf_op jit(solution)/shard_map/all_to_all | solution.py:314
  63.3 0.2 collective-permute-start
  63.6 3.9 %collective-permute-done.other_ref = bf16[1024,896]{1,0:T(8,128)(2,1)} collective-permute-done((bf16[1024,896]{1,0:T(8,128)(2,1)S(1)}, bf16[1024,896]{1,0:T(8,128)(2,1)}, u32[]{:S(2)}, u32[]{:S(2)}) %collective-permute-start) | collective-permute-done | bytes 1835040 | tf_op jit(solution)/shard_map/ppermute | solution.py:307
  67.5 41.3 %pivot_factor.1 = (bf16[1024,1152]{1,0:T(8,128)(2,1)}, bf16[1024,1024]{1,0:T(8,128)(2,1)}, bf16[1024,1024]{1,0:T(8,128)(2,1)}) custom-call(s32[1]{0:T(128)} %bitcast.6.core_ref, bf16[1024,896]{1,0:T(8,128)(2,1)} %bitcast.17, bf16[1024,896]{1,0:T(8,128)(2,1)} %collective-permute-done.other_ref), custom_call_target="tpu_custom_call" | custom-call | tf_op jit(solution)/shard_map/pivot_factor/pallas_call | solution.py:155
  108.8 41.2 %final.1 = (f32[1024,1024]{1,0:T(8,128)}, f32[1024,2048]{1,0:T(8,128)}) custom-call(s32[2]{0:T(128)S(1)} %pad_add_fusion.at_ref, bf16[1024,1152]{1,0:T(8,128)(2,1)} %bitcast.5.rows_ref, bf16[1024,1152]{1,0:T(8,128)(2,1)} %get-tuple-element.5.pivots_ref, bf16[1024,1024]{1,0:T(8,128)(2,1)} %get-tuple-element.6.high_ref, ...), custom_call_target="tpu_custom_call" | custom-call | tf_op jit(solution)/shard_map/final/pallas_call | solution.py:231
  (34 shorter events, 0.8 us)
Async XLA Ops:
  7.2 1.2 copy-start
  7.2 101.6 %all-gather.2.cloned.1.call-start = ((), (), s32[]{:S(2)}) async-start(), calls=%async_computation.2 | async-start | bytes 4456448 | tf_op jit(solution)/shard_map/all_gather | solution.py:312
  8.4 4.8 %copy-start.2 = (s32[1024]{0:T(1024)S(1)}, s32[1024]{0:T(1024)}, u32[]{:S(2)}) copy-start(s32[1024]{0:T(1024)} %param.9) | copy-start | bytes 12292
  8.4 4.8 %copy-start.3 = (s32[128]{0:T(128)S(1)}, s32[128]{0:T(128)}, u32[]{:S(2)}) copy-start(s32[128]{0:T(128)} %param.8) | copy-start | bytes 1540
  8.4 5.2 %copy-start.4 = (s32[8]{0:T(128)S(1)}, s32[8]{0:T(128)}, u32[]{:S(2)}) copy-start(s32[8]{0:T(128)} %constant.99.clone.1) | copy-start | bytes 100
  54.3 9.0 %copy-start.1 = (bf16[128,8,896]{2,1,0:T(8,128)(2,1)}, bf16[128,8,896]{2,1,0:T(8,128)(2,1)S(1)}, u32[]{:S(2)}) copy-start(bf16[128,8,896]{2,1,0:T(8,128)(2,1)S(1)} %all_to_all.10) | copy-start | bytes 5505028
  57.7 51.1 %all-to-all-start.1 = ((bf16[8,128,1152]{2,1,0:T(8,128)(2,1)}), bf16[8,128,1152]{2,1,0:T(8,128)(2,1)}, u32[]{:S(2)}, u32[]{:S(2)}) async-start(bf16[8,128,1152]{2,1,0:T(8,128)(2,1)} %broadcast_in_dim.199), calls=%async_computation.1 | async-start | bytes 4718592 | tf_op jit(solution)/shard_map/all_to_all | solution.py:314
  63.3 4.2 %collective-permute-start = (bf16[1024,896]{1,0:T(8,128)(2,1)S(1)}, bf16[1024,896]{1,0:T(8,128)(2,1)}, u32[]{:S(2)}, u32[]{:S(2)}) collective-permute-start(bf16[1024,896]{1,0:T(8,128)(2,1)S(1)} %bitcast.16), channel_id=1, source_target_pairs={{0,1},{1,0},{2,3},{3,2},{4,5},{5,4},{6,7},{7,6},{8,9},{9,8},{10,11... | collective-permute-start | bytes 5505032 | tf_op jit(solution)/shard_map/ppermute | solution.py:307
Sparse Core Ops, SparseCore 0:
  55.8 47.1 all-gather.1
